TPU v7x, 1024 devices: a whole 8x8x8 slice. The times are simulated.
1024 devices in a mesh: node: 128 (over y, z, core), local: 8 (over x).
Axes of the slice: x: 8, y: 8, z: 8, core: 2. Of those that a mesh axis runs over, the one named last changes fastest.
Arguments:
- tokens: bfloat16 [4096, 4096], P('node', 'local'), may hold values from -6 to 6
- node_ids: int32 [4096, 4], P('node'), may hold values from 0 to 127, all different within a row; in each aligned block of 32 rows (0 to 31, 32 to 63, ...) at most 2 rows name the same one
- mix_weights: float32 [4096, 4], P('node'), may hold values from 0.05 to 1
- w_gate: bfloat16 [128, 4096, 1024], P('node', 'local'), may hold values from -0.09375 to 0.09375
- w_up: bfloat16 [128, 4096, 1024], P('node', 'local'), may hold values from -0.09375 to 0.09375
- w_down: bfloat16 [128, 1024, 4096], P('node', None, 'local'), may hold values from -0.1875 to 0.1875
Outputs:
- mixed: bfloat16 [4096, 4096], P('node', 'local')
Inputs may be any that keep to these rules, and one draw needn't show every extreme that they name: `node_ids`: each row names 4 different experts. Among the 32 tokens of one node (aligned blocks of rows), at most 2 name the same expert, and in every draw some expert is named by exactly 2 tokens of some node.
All inputs are finite; a program needn't handle non-finite values.
Results may differ from a plain program's by a relative error of at most 0.023.
Values may be sent and summed in bfloat16 or wider, within the bound.
No kernel may reach another device: no remote copies, remote signals or barrier semaphores. Data moves between devices by JAX's collectives and lax.ppermute only.
A program may use at most 32 MiB of HBM per device.

v0:
```python
import jax
import jax.numpy as jnp
from jax import lax
from jax.sharding import PartitionSpec as P


def body(tokens, node_ids, mix_weights, w_gate, w_up, w_down):
    row_count, feat_width = tokens.shape
    pick_count = node_ids.shape[1]
    node_count = lax.axis_size("node")
    slot_cap = max(2, 2 * row_count * pick_count // node_count)
    slot_total = node_count * slot_cap
    flat_ids = node_ids.reshape(-1)
    hit_table = (flat_ids[:, None] == jnp.arange(node_count, dtype=jnp.int32)[None, :]).astype(
        jnp.int32
    )
    earlier = jnp.cumsum(hit_table, axis=0) - hit_table
    slot_rank = jnp.sum(earlier * hit_table, axis=1)
    position = flat_ids * slot_cap + slot_rank
    slot_table = jnp.arange(slot_total, dtype=jnp.int32)[:, None] == position[None, :]
    dispatch = jnp.any(slot_table.reshape(slot_total, row_count, pick_count), axis=2).astype(
        jnp.bfloat16
    )
    outbound = jnp.dot(dispatch, tokens, preferred_element_type=jnp.float32).astype(jnp.bfloat16)
    outbound = outbound.reshape(node_count, slot_cap, feat_width)
    inbound = lax.all_to_all(outbound, "node", split_axis=0, concat_axis=0, tiled=True)
    inbound = inbound.reshape(slot_total, feat_width)
    gate_part = jnp.dot(inbound, w_gate[0], preferred_element_type=jnp.float32)
    up_part = jnp.dot(inbound, w_up[0], preferred_element_type=jnp.float32)
    gate_share, up_share = (
        lax.psum_scatter(
            gate_part.astype(jnp.bfloat16), "local", scatter_dimension=1, tiled=True
        ).astype(jnp.float32),
        lax.psum_scatter(
            up_part.astype(jnp.bfloat16), "local", scatter_dimension=1, tiled=True
        ).astype(jnp.float32),
    )
    active = (jax.nn.silu(gate_share) * up_share).astype(jnp.bfloat16)
    down_rows = w_down[0]
    result = jnp.dot(
        lax.all_gather(active, "local", axis=1, tiled=True),
        down_rows,
        preferred_element_type=jnp.float32,
    )
    expert_out = result.astype(jnp.bfloat16).reshape(node_count, slot_cap, feat_width)
    returned = lax.all_to_all(expert_out, "node", split_axis=0, concat_axis=0, tiled=True)
    returned = returned.reshape(slot_total, feat_width)
    weighting = slot_table.astype(jnp.float32) * mix_weights.reshape(-1)[None, :]
    combine = jnp.sum(weighting.reshape(slot_total, row_count, pick_count), axis=2)
    mixed = lax.dot_general(
        combine,
        returned.astype(jnp.float32),
        (((0,), (0,)), ((), ())),
        precision=lax.Precision.HIGHEST,
    )
    return mixed.astype(jnp.bfloat16)


def solution(mesh):
    return jax.shard_map(
        body,
        mesh=mesh,
        in_specs=(
            P("node", "local"),
            P("node", None),
            P("node", None),
            P("node", "local", None),
            P("node", "local", None),
            P("node", None, "local"),
        ),
        out_specs=P("node", "local"),
        check_vma=False,
    )
```

profile of v0, /device:TPU:1, one launch (start us, length us, event | category | flops | bytes accessed | tf_op | source)
XLA Modules:
  0.0 194.7 jit_solution(16554513091472358211)
XLA Ops:
  6.5 0.0 copy-start
  6.5 0.0 reduce-scatter.7.cloned.1.call-start
  6.5 0.8 copy.23
  7.4 0.1 eq.31
  7.5 0.1 fusion.9
  7.6 0.2 reduce_window_sum.11
  7.8 0.2 select_reduce_fusion.1
  7.9 0.0 copy-start.3
  8.0 0.1 reduce_sum.21
  8.1 0.0 copy-start.4
  8.1 0.1 copy.24
  8.1 0.6 copy-done.4
  8.7 0.1 fusion.7
  8.8 0.0 copy-done.3
  8.9 0.3 convolution_convert_fusion.2
  9.1 0.1 reshape.46
  9.2 39.3 %all_to_all.10 = bf16[128,2,512]{2,1,0:T(2,128)(2,1)S(1)} all-to-all(bf16[128,2,512]{2,1,0:T(2,128)(2,1)S(1)} %reshape.46), channel_id=1, replica_groups=mesh['node'=128,'local'=8] {'node'}, dimensions={0} | all-to-all | bytes 524288 | tf_op jit(solution)/shard_map/all_to_all | solution.py:26
  48.6 0.1 reshape.47
  48.7 0.0 copy-done
  48.7 0.4 convolution_convert_fusion.1
  49.1 0.0 copy-start.1
  49.2 1.0 copy.25
  50.2 0.0 reduce-scatter.7.cloned.1.call-update
  50.2 0.0 reduce-scatter.9.cloned.1.call-start
  50.2 0.3 copy-done.1
  50.6 0.4 convolution_convert_fusion
  51.0 1.0 copy.27
  52.0 0.0 copy-start.2
  52.0 0.0 reduce-scatter.9.cloned.1.call-update
  52.0 28.6 %reduce-scatter.7.cloned.1.call-done = bf16[128,256]{1,0:T(8,128)(2,1)} async-done(((bf16[1024,256]{1,0:T(8,128)(2,1)}), bf16[128,256]{1,0:T(8,128)(2,1)}) %reduce-scatter.7.cloned.1.call-update) | async-done | bytes 65552
  80.6 0.9 copy.26
  81.6 44.8 %reduce-scatter.9.cloned.1.call-done = bf16[128,256]{1,0:T(8,128)(2,1)} async-done(((bf16[1024,256]{1,0:T(8,128)(2,1)}), bf16[128,256]{1,0:T(8,128)(2,1)}) %reduce-scatter.9.cloned.1.call-update) | async-done | bytes 65552
  126.3 0.9 copy.28
  127.3 0.1 fusion.8
  127.3 18.8 %all_gather.3 = bf16[256,1024]{1,0:T(8,128)(2,1)S(1)} all-gather(bf16[256,128]{1,0:T(8,128)(2,1)S(1)} %fusion.8), channel_id=1, replica_groups=mesh['node'=128,'local'=8] {'local'}, dimensions={1}, use_global_device_ids=true | all-gather | bytes 589824 | tf_op jit(solution)/shard_map/all_gather | solution.py:41
  146.1 0.0 copy-done.2
  146.1 0.4 convolution_convert_fusion.3
  146.6 0.8 reshape.48
  147.4 0.0 copy-start.5
  147.4 25.3 %all-to-all-start.1 = ((bf16[128,2,512]{2,1,0:T(2,128)(2,1)}), bf16[128,2,512]{2,1,0:T(2,128)(2,1)S(1)}, u32[]{:S(2)}, u32[]{:S(2)}) async-start(bf16[128,2,512]{2,1,0:T(2,128)(2,1)} %reshape.48), calls=%async_computation.1 | async-start | bytes 524288 | tf_op jit(solution)/shard_map/all_to_all | solution.py:46
  172.7 0.0 copy-done.5
  172.7 0.1 select_reduce_fusion
  172.8 14.1 %all-to-all-done.1 = bf16[128,2,512]{2,1,0:T(2,128)(2,1)S(1)} async-done(((bf16[128,2,512]{2,1,0:T(2,128)(2,1)}), bf16[128,2,512]{2,1,0:T(2,128)(2,1)S(1)}, u32[]{:S(2)}, u32[]{:S(2)}) %all-to-all-start.1) | async-done | bytes 262176 | tf_op jit(solution)/shard_map/all_to_all | solution.py:46
  186.9 0.1 reshape.49
  187.0 0.9 convolution_convert_fusion.4
  (1 shorter events, 0.0 us)
Async XLA Ops:
  6.5 42.1 %copy-start = (bf16[1,512,1024]{2,1,0:T(8,128)(2,1)S(1)}, bf16[1,512,1024]{2,1,0:T(8,128)(2,1)}, u32[]{:S(2)}) copy-start(bf16[1,512,1024]{2,1,0:T(8,128)(2,1)} %param.9) | copy-start | bytes 3145732
  6.5 74.1 %reduce-scatter.7.cloned.1.call-start = ((), (), s32[]{:S(2)}) async-start(), calls=%async_computation.4 | async-start | bytes 589824
  7.9 0.9 copy-start.3
  8.1 0.7 copy-start.4
  49.1 1.4 copy-start.1
  50.2 76.1 %reduce-scatter.9.cloned.1.call-start = ((), (), s32[]{:S(2)}) async-start(), calls=%async_computation.5 | async-start | bytes 589824
  52.0 94.1 %copy-start.2 = (bf16[1,1024,512]{2,1,0:T(8,128)(2,1)S(1)}, bf16[1,1024,512]{2,1,0:T(8,128)(2,1)}, u32[]{:S(2)}) copy-start(bf16[1,1024,512]{2,1,0:T(8,128)(2,1)} %param.11) | copy-start | bytes 3145732
  147.4 25.3 %copy-start.5 = (f32[32,4]{0,1:T(4,128)S(1)}, f32[32,4]{0,1:T(4,128)}, u32[]{:S(2)}) copy-start(f32[32,4]{0,1:T(4,128)} %param.8) | copy-start | bytes 1540
  147.4 39.5 %all-to-all-start.1 = ((bf16[128,2,512]{2,1,0:T(2,128)(2,1)}), bf16[128,2,512]{2,1,0:T(2,128)(2,1)S(1)}, u32[]{:S(2)}, u32[]{:S(2)}) async-start(bf16[128,2,512]{2,1,0:T(2,128)(2,1)} %reshape.48), calls=%async_computation.1 | async-start | bytes 524288 | tf_op jit(solution)/shard_map/all_to_all | solution.py:46
Sparse Core Ops, SparseCore 0:
  50.3 30.2 reduce-scatter.6
  84.0 42.2 reduce-scatter.8
where the time goes:
time: 195 us
  waiting for transfers between devices  87.5 us (45%)
  blocking collectives  58.1 us (30%)
  starting transfers between devices  25.3 us (13%)
  between operations  13.6 us (7%)
  local copies, waits for them, and re-layouts  7.07 us (4%)
  matrix products  2.45 us (1%)
    unnamed x4, waiting for transfers between devices  73.4 us
    all_to_all x1, blocking collectives, body(): lax.all_to_all(outbound, 'node', split_axis=0, concat_axis=0, tiled=True)  39.3 us
    all_to_all x1, starting transfers between devices, body(): lax.all_to_all(expert_out, 'node', split_axis=0, concat_axis=0, tiled=True)  25.3 us
    all_gather x1, blocking collectives, body(): lax.all_gather(active, 'local', axis=1, tiled=True)  18.8 us
    all_to_all x1, waiting for transfers between devices, body(): lax.all_to_all(expert_out, 'node', split_axis=0, concat_axis=0, tiled=True)  14.1 us
    unnamed x17, local copies, waits for them, and re-layouts  5.7 us
  transfers between devices with their start and end apart: 3, of which 3 were waited for; matrix products, arithmetic and copies ran while one was open for 1% of the time, Pallas kernels for 0%

commit v1 on v0

v1 whole, which is shorter than its diff:
```python
import jax
import jax.numpy as jnp
from jax import lax
from jax.sharding import PartitionSpec as P


def body(tokens, node_ids, mix_weights, w_gate, w_up, w_down):
    row_count, feat_width = tokens.shape
    node_count = lax.axis_size("node")
    local_count = lax.axis_size("local")
    hidden = w_gate.shape[2]
    cap = 2
    slots = node_count * cap
    share = slots // local_count

    experts = jnp.arange(node_count, dtype=jnp.int32)
    match = node_ids.T[:, None, :] == experts[None, :, None]
    hit = jnp.any(match, axis=0)
    weight = jnp.sum(jnp.where(match, mix_weights.T[:, None, :], 0.0), axis=0)
    earlier = jnp.arange(row_count)[:, None] < jnp.arange(row_count)[None, :]
    rank = jnp.dot(
        hit.astype(jnp.bfloat16), earlier.astype(jnp.bfloat16), preferred_element_type=jnp.float32
    )
    picked = hit[:, None, :] & (rank[:, None, :] == jnp.arange(cap, dtype=jnp.float32)[None, :, None])
    dispatch = picked.reshape(slots, row_count).astype(jnp.bfloat16)
    combine = jnp.where(picked, weight[:, None, :], 0.0).reshape(slots, row_count)

    outbound = jnp.dot(dispatch, tokens, preferred_element_type=jnp.float32).astype(jnp.bfloat16)
    inbound = lax.all_to_all(
        outbound.reshape(node_count, cap, feat_width), "node", split_axis=0, concat_axis=0, tiled=True
    ).reshape(slots, feat_width)

    gate_part = jnp.dot(inbound, w_gate[0], preferred_element_type=jnp.float32).astype(jnp.bfloat16)
    up_part = jnp.dot(inbound, w_up[0], preferred_element_type=jnp.float32).astype(jnp.bfloat16)
    parts = jnp.concatenate([gate_part, up_part], axis=1).reshape(local_count, share, 2 * hidden)
    parts = lax.all_to_all(parts, "local", split_axis=0, concat_axis=0, tiled=True)
    total = jnp.sum(parts.astype(jnp.float32), axis=0)
    active = (jax.nn.silu(total[:, :hidden]) * total[:, hidden:]).astype(jnp.bfloat16)

    copies = jnp.broadcast_to(active[None], (local_count, share, hidden))
    rows = lax.all_to_all(copies, "local", split_axis=0, concat_axis=0, tiled=True)
    result = jnp.dot(
        rows.reshape(slots, hidden), w_down[0], preferred_element_type=jnp.float32
    ).astype(jnp.bfloat16)
    returned = lax.all_to_all(
        result.reshape(node_count, cap, feat_width), "node", split_axis=0, concat_axis=0, tiled=True
    ).reshape(slots, feat_width)
    mixed = lax.dot_general(
        combine,
        returned.astype(jnp.float32),
        (((0,), (0,)), ((), ())),
        precision=lax.Precision.HIGHEST,
    )
    return mixed.astype(jnp.bfloat16)


def solution(mesh):
    return jax.shard_map(
        body,
        mesh=mesh,
        in_specs=(
            P("node", "local"),
            P("node", None),
            P("node", None),
            P("node", "local", None),
            P("node", "local", None),
            P("node", None, "local"),
        ),
        out_specs=P("node", "local"),
        check_vma=False,
    )
```

time: 195 us -> 122 us (0.63)
  waiting for transfers between devices: 87.5 us -> 13.9 us
  blocking collectives: 58.1 us -> 89.3 us
  starting transfers between devices: 25.3 us -> 10.7 us
  between operations: 13.6 us -> 0.18 us
  local copies, waits for them, and re-layouts: 7.07 us -> 2.4 us
    unnamed x4 -> x0, waiting for transfers between devices: 73.4 us -> none
    all_to_all x1 -> x3, blocking collectives: 39.3 us -> 89.3 us  [the longest x1 39.3 us: body(): lax.all_to_all(outbound.reshape(node_count, cap, feat_width), 'node', spl...]
    all_gather x1 -> x0, blocking collectives: 18.8 us -> none  [body(): lax.all_gather(active, 'local', axis=1, tiled=True)]
    all_to_all x1, starting transfers between devices: 25.3 us -> 10.7 us  [body(): lax.all_to_all(result.reshape(node_count, cap, feat_width), 'node', split...]
    unnamed x17 -> x10, local copies, waits for them, and re-layouts: 5.7 us -> 0.79 us
  transfers between devices with their start and end apart: 3 -> 1, of which waited for: 3 -> 1; matrix products, arithmetic and copies ran while one was open for 1% -> 0% of each run, Pallas kernels for 0% -> 0%
where the time goes in v1:
time: 122 us; the launch traced here: 121 us
  blocking collectives  89.3 us (73%)
  waiting for transfers between devices  13.9 us (11%)
  starting transfers between devices  10.7 us (9%)
  matrix products  3.44 us (3%)
  local copies, waits for them, and re-layouts  2.4 us (2%)
  other arithmetic  1.35 us (1%)
    all_to_all x1, blocking collectives, body(): lax.all_to_all(outbound.reshape(node_count, cap, feat_width), 'node', spl...  39.3 us
    all_to_all x1, blocking collectives, body(): lax.all_to_all(parts, 'local', split_axis=0, concat_axis=0, tiled=True)  32.2 us
    all_to_all x1, blocking collectives, body(): lax.all_to_all(copies, 'local', split_axis=0, concat_axis=0, tiled=True)  17.8 us
    all_to_all x1, waiting for transfers between devices, body(): lax.all_to_all(result.reshape(node_count, cap, feat_width), 'node', split...  13.9 us
    all_to_all x1, starting transfers between devices, body(): lax.all_to_all(result.reshape(node_count, cap, feat_width), 'node', split...  10.7 us
  transfers between devices with their start and end apart: 1, of which 1 were waited for; matrix products, arithmetic and copies ran while one was open for 0% of the time, Pallas kernels for 0%

profile of v1, /device:TPU:1, one launch (start us, length us, event | category | flops | bytes accessed | tf_op | source)
XLA Modules:
  0.0 121.2 jit_solution(16463408359000599251)
XLA Ops:
  0.0 0.0 copy-start
  0.0 0.9 fusion.10
  0.9 0.2 fusion.11
  1.1 0.1 copy.14
  1.2 0.1 and.13
  1.3 0.1 and.15
  1.4 0.1 eq.45
  1.6 1.0 convolution_convert_fusion.2
  2.6 0.1 reshape.27
  2.7 39.3 %all_to_all.20 = bf16[128,2,512]{2,1,0:T(2,128)(2,1)S(1)} all-to-all(bf16[128,2,512]{2,1,0:T(2,128)(2,1)S(1)} %reshape.27), channel_id=1, replica_groups=mesh['node'=128,'local'=8] {'node'}, dimensions={0} | all-to-all | bytes 524288 | tf_op jit(solution)/shard_map/all_to_all | solution.py:29
  42.1 0.1 reshape.28
  42.2 0.0 copy-done
  42.2 0.0 copy-start.1
  42.2 0.4 convolution_convert_fusion
  42.6 0.8 copy-done.1
  43.4 0.4 convolution_convert_fusion.1
  43.8 0.1 pad_maximum_fusion
  43.9 32.2 %all_to_all.21 = bf16[8,32,2048]{2,1,0:T(8,128)(2,1)S(1)} all-to-all(bf16[8,32,2048]{2,1,0:T(8,128)(2,1)S(1)} %bitcast.23), channel_id=1, replica_groups=mesh['node'=128,'local'=8] {'local'}, dimensions={0} | all-to-all | bytes 2097152 | tf_op jit(solution)/shard_map/all_to_all | solution.py:36
  76.1 0.1 convert_reduce_fusion
  76.3 0.0 copy-start.2
  76.3 0.1 broadcast_in_dim.43
  76.4 17.8 %all_to_all.22 = bf16[8,32,1024]{2,1,0:T(8,128)(2,1)S(1)} all-to-all(bf16[8,32,1024]{2,1,0:T(8,128)(2,1)S(1)} %broadcast_in_dim.43), channel_id=1, replica_groups=mesh['node'=128,'local'=8] {'local'}, dimensions={0} | all-to-all | bytes 1048576 | tf_op jit(solution)/shard_map/all_to_all | solution.py:41
  94.2 0.0 copy-done.2
  94.2 0.0 copy-start.3
  94.2 0.0 copy-start.4
  94.2 0.4 convolution_convert_fusion.3
  94.6 0.8 reshape.31
  95.4 10.7 %all-to-all-start.3 = ((bf16[128,2,512]{2,1,0:T(2,128)(2,1)}), bf16[128,2,512]{2,1,0:T(2,128)(2,1)S(1)}, u32[]{:S(2)}, u32[]{:S(2)}) async-start(bf16[128,2,512]{2,1,0:T(2,128)(2,1)} %reshape.31), calls=%async_computation.3 | async-start | bytes 524288 | tf_op jit(solution)/shard_map/all_to_all | solution.py:45
  106.1 0.0 copy-done.3
  106.1 0.0 copy-done.4
  106.1 0.1 select_reduce_fusion
  106.2 0.1 copy.16
  106.3 0.1 and_select_fusion
  106.4 13.9 %all-to-all-done.3 = bf16[128,2,512]{2,1,0:T(2,128)(2,1)S(1)} async-done(((bf16[128,2,512]{2,1,0:T(2,128)(2,1)}), bf16[128,2,512]{2,1,0:T(2,128)(2,1)S(1)}, u32[]{:S(2)}, u32[]{:S(2)}) %all-to-all-start.3) | async-done | bytes 262176 | tf_op jit(solution)/shard_map/all_to_all | solution.py:45
  120.3 0.9 fusion
  (3 shorter events, 0.1 us)
Async XLA Ops:
  0.0 42.2 %copy-start = (bf16[1,512,1024]{2,1,0:T(8,128)(2,1)S(1)}, bf16[1,512,1024]{2,1,0:T(8,128)(2,1)}, u32[]{:S(2)}) copy-start(bf16[1,512,1024]{2,1,0:T(8,128)(2,1)} %param.10) | copy-start | bytes 3145732
  42.2 1.2 %copy-start.1 = (bf16[1,512,1024]{2,1,0:T(8,128)(2,1)S(1)}, bf16[1,512,1024]{2,1,0:T(8,128)(2,1)}, u32[]{:S(2)}) copy-start(bf16[1,512,1024]{2,1,0:T(8,128)(2,1)} %param.9) | copy-start | bytes 3145732
  76.3 17.9 %copy-start.2 = (bf16[1,1024,512]{2,1,0:T(8,128)(2,1)S(1)}, bf16[1,1024,512]{2,1,0:T(8,128)(2,1)}, u32[]{:S(2)}) copy-start(bf16[1,1024,512]{2,1,0:T(8,128)(2,1)} %param.11) | copy-start | bytes 3145732
  94.2 11.9 %copy-start.3 = (s32[32,4]{0,1:T(4,128)S(1)}, s32[32,4]{0,1:T(4,128)}, u32[]{:S(2)}) copy-start(s32[32,4]{0,1:T(4,128)} %param.7) | copy-start | bytes 1540
  94.2 11.9 %copy-start.4 = (f32[32,4]{0,1:T(4,128)S(1)}, f32[32,4]{0,1:T(4,128)}, u32[]{:S(2)}) copy-start(f32[32,4]{0,1:T(4,128)} %param.8) | copy-start | bytes 1540
  95.4 24.9 %all-to-all-start.3 = ((bf16[128,2,512]{2,1,0:T(2,128)(2,1)}), bf16[128,2,512]{2,1,0:T(2,128)(2,1)S(1)}, u32[]{:S(2)}, u32[]{:S(2)}) async-start(bf16[128,2,512]{2,1,0:T(2,128)(2,1)} %reshape.31), calls=%async_computation.3 | async-start | bytes 524288 | tf_op jit(solution)/shard_map/all_to_all | solution.py:45

commit v2 on v1

v2 whole, which is shorter than its diff:
```python
import jax
import jax.numpy as jnp
import numpy as np
from jax import lax
from jax.sharding import PartitionSpec as P

CAP = 2
CORES = 2
BOTH = ("node", "local")
FIRST = (0, 2, 5, 7)
SECOND = (1, 3, 4, 6)
TEAM = (0, 1, 0, 1, 1, 0, 1, 0)


def seat(label, core):
    return (label + core) % 8


def body(tokens, node_ids, mix_weights, w_gate, w_up, w_down):
    row_count, feat_width = tokens.shape
    node_count = lax.axis_size("node")
    local_count = lax.axis_size("local")
    hidden = w_gate.shape[2]
    chips = node_count // CORES
    slots = node_count * CAP
    half = slots // 2
    share = slots // local_count

    chip_groups = [[chip * CORES + core for chip in range(chips)] for core in range(CORES)]
    core_swap = [(node, node ^ 1) for node in range(node_count)]
    team_groups = [
        [node * local_count + seat(label, node % CORES) for label in team]
        for node in range(node_count)
        for team in (FIRST, SECOND)
    ]
    pair_swap = [
        (node * local_count + seat(label, node % CORES), node * local_count + seat(label ^ 1, node % CORES))
        for node in range(node_count)
        for label in range(local_count)
    ]
    core = lax.axis_index("node") % CORES
    team = jnp.asarray(np.array(TEAM, np.int32))[(lax.axis_index("local") + local_count - core) % local_count]

    def exchange(array, axis, groups):
        return lax.all_to_all(
            array, axis, split_axis=0, concat_axis=0, tiled=True, axis_index_groups=groups
        )

    chip_index = jnp.arange(chips, dtype=jnp.int32) * CORES
    experts = jnp.concatenate([chip_index + core, chip_index + 1 - core])
    match = node_ids.T[:, None, :] == experts[None, :, None]
    hit = jnp.any(match, axis=0)
    weight = jnp.sum(jnp.where(match, mix_weights.T[:, None, :], 0.0), axis=0)
    earlier = jnp.arange(row_count)[:, None] < jnp.arange(row_count)[None, :]
    rank = jnp.dot(
        hit.astype(jnp.bfloat16), earlier.astype(jnp.bfloat16), preferred_element_type=jnp.float32
    )
    picked = hit[:, None, :] & (rank[:, None, :] == jnp.arange(CAP, dtype=jnp.float32)[None, :, None])
    dispatch = picked.reshape(slots, row_count).astype(jnp.bfloat16)
    combine = jnp.where(picked, weight[:, None, :], 0.0).reshape(slots, row_count)

    outbound = jnp.dot(dispatch, tokens, preferred_element_type=jnp.float32).astype(jnp.bfloat16)
    theirs = lax.ppermute(outbound[half:], "node", core_swap)
    mine = outbound[:half].reshape(chips, CAP, feat_width)
    leaving = jnp.concatenate([mine, theirs.reshape(chips, CAP, feat_width)], axis=1)
    inbound = exchange(leaving, "node", chip_groups).reshape(2, half, feat_width)

    def project(rows):
        gate = jnp.dot(rows, w_gate[0], preferred_element_type=jnp.float32)
        up = jnp.dot(rows, w_up[0], preferred_element_type=jnp.float32)
        return gate, up

    first_team = team == 0
    away = jnp.where(first_team, inbound[1], inbound[0])
    kept = jnp.where(first_team, inbound[0], inbound[1])
    gate_away, up_away = project(away)
    sent = jnp.concatenate([gate_away.astype(jnp.bfloat16), up_away.astype(jnp.bfloat16)], axis=1)
    got = lax.ppermute(sent, BOTH, pair_swap)
    gate_kept, up_kept = project(kept)
    pair = jnp.concatenate(
        [
            (gate_kept + got[:, :hidden].astype(jnp.float32)).astype(jnp.bfloat16),
            (up_kept + got[:, hidden:].astype(jnp.float32)).astype(jnp.bfloat16),
        ],
        axis=1,
    )
    parts = exchange(pair.reshape(half // share, share, 2 * hidden), BOTH, team_groups)
    total = jnp.sum(parts.astype(jnp.float32), axis=0)
    active = (jax.nn.silu(total[:, :hidden]) * total[:, hidden:]).astype(jnp.bfloat16)

    copies = jnp.broadcast_to(active[None], (half // share, share, hidden))
    own = exchange(copies, BOTH, team_groups).reshape(half, hidden)
    other = lax.ppermute(own, BOTH, pair_swap)
    own_out = jnp.dot(own, w_down[0], preferred_element_type=jnp.float32).astype(jnp.bfloat16)
    other_out = jnp.dot(other, w_down[0], preferred_element_type=jnp.float32).astype(jnp.bfloat16)
    result = jnp.concatenate(
        [jnp.where(first_team, own_out, other_out), jnp.where(first_team, other_out, own_out)], axis=0
    )
    returned = exchange(result.reshape(chips, CORES * CAP, feat_width), "node", chip_groups)
    swapped = lax.ppermute(returned[:, CAP:].reshape(half, feat_width), "node", core_swap)

    def weigh(weights, rows):
        return lax.dot_general(
            weights,
            rows.astype(jnp.float32),
            (((0,), (0,)), ((), ())),
            precision=lax.Precision.HIGHEST,
        )

    mixed = weigh(combine[:half], returned[:, :CAP].reshape(half, feat_width))
    mixed = mixed + weigh(combine[half:], swapped)
    return mixed.astype(jnp.bfloat16)


def solution(mesh):
    return jax.shard_map(
        body,
        mesh=mesh,
        in_specs=(
            P("node", "local"),
            P("node", None),
            P("node", None),
            P("node", "local", None),
            P("node", "local", None),
            P("node", None, "local"),
        ),
        out_specs=P("node", "local"),
        check_vma=False,
    )
```

time: 122 us -> 123 us (level)
  blocking collectives: 89.3 us -> 23.7 us
  starting transfers between devices: 10.7 us -> 52.7 us
  waiting for transfers between devices: 13.9 us -> 34.1 us
  local copies, waits for them, and re-layouts: 2.4 us -> 5.63 us
    all_to_all x3 -> x2, blocking collectives: 89.3 us -> 23.7 us  [exchange(): lax.all_to_all(array, axis, split_axis=0, concat_axis=0, tiled=True, axis...]
    ppermute x0 -> x4, starting transfers between devices: none -> 35.9 us  [the longest x1 16 us: body(): theirs = lax.ppermute(outbound[half:], 'node', core_swap)]
    ppermute x0 -> x4, waiting for transfers between devices: none -> 11.1 us  [the longest x1 6.27 us: body(): got = lax.ppermute(sent, BOTH, pair_swap)]
    all_to_all x1 -> x2, waiting for transfers between devices: 13.9 us -> 23 us  [exchange(): lax.all_to_all(array, axis, split_axis=0, concat_axis=0, tiled=True, axis...]
    all_to_all x1 -> x2, starting transfers between devices: 10.7 us -> 16.9 us  [exchange(): lax.all_to_all(array, axis, split_axis=0, concat_axis=0, tiled=True, axis...]
    unnamed x10 -> x26, local copies, waits for them, and re-layouts: 0.79 us -> 3.32 us
    dot_general x4 -> x8, matrix products: 2.2 us -> 2.94 us  [the longest x2 1.09 us: weigh(): lax.dot_general(weights, rows.astype(jnp.float32), (((0,), (0,)), ((), ()...]
  transfers between devices with their start and end apart: 1 -> 6, of which waited for: 1 -> 6; matrix products, arithmetic and copies ran while one was open for 0% -> 1% of each run, Pallas kernels for 0% -> 0%
where the time goes in v2:
time: 123 us; the launch traced here: 122 us
  starting transfers between devices  52.7 us (43%)
  waiting for transfers between devices  34.1 us (28%)
  blocking collectives  23.7 us (19%)
  local copies, waits for them, and re-layouts  5.63 us (5%)
  matrix products  3.4 us (3%)
  other arithmetic  1.56 us (1%)
    all_to_all x2, blocking collectives, exchange(): lax.all_to_all(array, axis, split_axis=0, concat_axis=0, tiled=True, axis...  23.7 us
    all_to_all x2, waiting for transfers between devices, exchange(): lax.all_to_all(array, axis, split_axis=0, concat_axis=0, tiled=True, axis...  23 us
    all_to_all x2, starting transfers between devices, exchange(): lax.all_to_all(array, axis, split_axis=0, concat_axis=0, tiled=True, axis...  16.9 us
    ppermute x1, starting transfers between devices, body(): theirs = lax.ppermute(outbound[half:], 'node', core_swap)  16 us
    ppermute x1, starting transfers between devices, body(): lax.ppermute(returned[:, CAP:].reshape(half, feat_width), 'node', core_swap)  7.79 us
    ppermute x1, starting transfers between devices, body(): other = lax.ppermute(own, BOTH, pair_swap)  7.55 us
    ppermute x1, waiting for transfers between devices, body(): got = lax.ppermute(sent, BOTH, pair_swap)  6.27 us
    ppermute x1, starting transfers between devices, body(): got = lax.ppermute(sent, BOTH, pair_swap)  4.5 us
  transfers between devices with their start and end apart: 6, of which 6 were waited for; matrix products, arithmetic and copies ran while one was open for 1% of the time, Pallas kernels for 0%

profile of v2, /device:TPU:1, one launch (start us, length us, event | category | flops | bytes accessed | tf_op | source)
XLA Modules:
  0.0 122.1 jit_solution(3087404795768033518)
XLA Ops:
  0.0 0.0 copy-start
  0.0 0.0 copy-start.6
  0.0 0.1 pad_add_fusion
  0.1 0.0 copy-start.9
  0.1 0.6 copy-done.9
  0.7 0.1 copy-done.6
  0.8 0.1 compare_reduce_fusion
  0.9 0.0 copy-start.3
  0.9 0.2 fusion.18
  1.1 0.4 copy-done.3
  1.5 0.1 copy.24
  1.6 0.1 copy.25
  1.7 0.1 and.25.clone
  1.8 0.1 and.28
  1.9 0.1 eq.56
  2.0 0.0 copy-start.5
  2.1 0.7 copy-done.5
  2.8 0.3 convolution_convert_fusion
  3.1 16.0 %collective-permute-start = (bf16[128,512]{1,0:T(8,128)(2,1)S(1)}, bf16[128,512]{1,0:T(8,128)(2,1)S(1)}, u32[]{:S(2)}, u32[]{:S(2)}) collective-permute-start(bf16[128,512]{1,0:T(8,128)(2,1)S(1)} %get-tuple-element.14), channel_id=1, source_target_pairs={{0,8},{8,0},{16,24},{24,16},{32,40},{40,32},{48,56},{56,48},{64,72... | collective-permute-start | bytes 393224 | tf_op jit(solution)/shard_map/ppermute | solution.py:63
  19.1 0.1 reshape.44
  19.2 0.0 copy-start.2
  19.2 0.9 collective-permute-done
  20.1 0.1 reshape.45
  20.1 1.0 pad_maximum_fusion.2
  21.1 10.5 %all-to-all-start = ((bf16[64,4,512]{2,1,0:T(4,128)(2,1)}), bf16[64,4,512]{2,1,0:T(4,128)(2,1)S(1)}, u32[]{:S(2)}, u32[]{:S(2)}) async-start(bf16[64,4,512]{2,1,0:T(4,128)(2,1)} %pad_maximum_fusion.2), calls=%async_computation | async-start | bytes 524288 | tf_op jit(solution)/shard_map/all_to_all | solution.py:45
  31.6 0.0 copy-start.11
  31.6 0.6 copy-done.11
  32.3 0.6 dynamic_slice.3
  33.4 11.3 %all-to-all-done = bf16[64,4,512]{2,1,0:T(4,128)(2,1)S(1)} async-done(((bf16[64,4,512]{2,1,0:T(4,128)(2,1)}), bf16[64,4,512]{2,1,0:T(4,128)(2,1)S(1)}, u32[]{:S(2)}, u32[]{:S(2)}) %all-to-all-start) | async-done | bytes 262176 | tf_op jit(solution)/shard_map/all_to_all | solution.py:45
  44.7 0.1 broadcast_select_fusion
  44.8 0.0 copy-done.2
  44.9 0.3 convolution_convert_fusion.1
  45.2 0.0 copy-done
  45.2 0.3 convolution_convert_fusion.2
  45.5 4.5 %collective-permute-start.1 = (bf16[128,2048]{1,0:T(8,128)(2,1)S(1)}, bf16[128,2048]{1,0:T(8,128)(2,1)S(1)}, u32[]{:S(2)}, u32[]{:S(2)}) collective-permute-start(bf16[128,2048]{1,0:T(8,128)(2,1)S(1)} %pad_maximum_fusion), channel_id=1, source_target_pairs={{0,1},{1,0},{2,3},{3,2},{4,5},{5,4},{6,7},{7,6},{9,10},{10,9},{11,... | collective-permute-start | bytes 1572872 | tf_op jit(solution)/shard_map/ppermute | solution.py:78
  50.1 0.3 fusion.3
  50.4 6.3 %collective-permute-done.1 = bf16[128,2048]{1,0:T(8,128)(2,1)S(1)} collective-permute-done((bf16[128,2048]{1,0:T(8,128)(2,1)S(1)}, bf16[128,2048]{1,0:T(8,128)(2,1)S(1)}, u32[]{:S(2)}, u32[]{:S(2)}) %collective-permute-start.1) | collective-permute-done | bytes 524320 | tf_op jit(solution)/shard_map/ppermute | solution.py:78
  56.7 0.3 add_convert_fusion.1
  57.0 13.9 %all_to_all.20 = bf16[4,32,2048]{2,1,0:T(8,128)(2,1)S(1)} all-to-all(bf16[4,32,2048]{2,1,0:T(8,128)(2,1)S(1)} %bitcast.38), channel_id=1, replica_groups={{0,2,5,7},{1,3,4,6},{9,11,14,8},{10,12,13,15},{16,18,21,23},{17,19,20,2..., dimensions={0} | all-to-all | bytes 1048576 | tf_op jit(solution)/shard_map/all_to_all | solution.py:45
  71.0 0.1 convert_reduce_fusion
  71.1 9.8 %all_to_all.21 = bf16[4,32,1024]{2,1,0:T(8,128)(2,1)S(1)} all-to-all(bf16[4,32,1024]{2,1,0:T(8,128)(2,1)S(1)} %broadcast_in_dim.43), channel_id=1, replica_groups={{0,2,5,7},{1,3,4,6},{9,11,14,8},{10,12,13,15},{16,18,21,23},{17,19,20,2..., dimensions={0} | all-to-all | bytes 524288 | tf_op jit(solution)/shard_map/all_to_all | solution.py:45
  80.9 7.5 %collective-permute-start.2 = (bf16[128,1024]{1,0:T(8,128)(2,1)S(1)}, bf16[128,1024]{1,0:T(8,128)(2,1)S(1)}, u32[]{:S(2)}, u32[]{:S(2)}) collective-permute-start(bf16[128,1024]{1,0:T(8,128)(2,1)S(1)} %bitcast.39), channel_id=1, source_target_pairs={{0,1},{1,0},{2,3},{3,2},{4,5},{5,4},{6,7},{7,6},{9,10},{10,9},{11,... | collective-permute-start | bytes 786440 | tf_op jit(solution)/shard_map/ppermute | solution.py:93
  88.5 0.0 copy-done.1
  88.5 0.3 convolution_convert_fusion.4
  88.8 3.4 %collective-permute-done.2 = bf16[128,1024]{1,0:T(8,128)(2,1)S(1)} collective-permute-done((bf16[128,1024]{1,0:T(8,128)(2,1)S(1)}, bf16[128,1024]{1,0:T(8,128)(2,1)S(1)}, u32[]{:S(2)}, u32[]{:S(2)}) %collective-permute-start.2) | collective-permute-done | bytes 262176 | tf_op jit(solution)/shard_map/ppermute | solution.py:93
  92.2 0.3 broadcast_select_fusion.3
  92.6 0.8 reshape.48
  93.3 6.4 %all-to-all-start.3 = ((bf16[64,4,512]{2,1,0:T(4,128)(2,1)}), bf16[64,4,512]{2,1,0:T(4,128)(2,1)S(1)}, u32[]{:S(2)}, u32[]{:S(2)}) async-start(bf16[64,4,512]{2,1,0:T(4,128)(2,1)} %reshape.48), calls=%async_computation.3 | async-start | bytes 524288 | tf_op jit(solution)/shard_map/all_to_all | solution.py:45
  99.7 0.0 copy-start.10
  99.7 0.0 copy-done.7
  99.7 0.0 copy-done.8
  99.7 0.6 copy-done.10
  100.4 0.1 fusion.13
  100.5 11.8 %all-to-all-done.3 = bf16[64,4,512]{2,1,0:T(4,128)(2,1)S(1)} async-done(((bf16[64,4,512]{2,1,0:T(4,128)(2,1)}), bf16[64,4,512]{2,1,0:T(4,128)(2,1)S(1)}, u32[]{:S(2)}, u32[]{:S(2)}) %all-to-all-start.3) | async-done | bytes 262176 | tf_op jit(solution)/shard_map/all_to_all | solution.py:45
  112.2 0.2 fusion.20
  112.4 0.0 copy-start.4
  112.4 0.1 reshape.49
  112.5 7.8 %collective-permute-start.3 = (bf16[128,512]{1,0:T(8,128)(2,1)S(1)}, bf16[128,512]{1,0:T(8,128)(2,1)S(1)}, u32[]{:S(2)}, u32[]{:S(2)}) collective-permute-start(bf16[128,512]{1,0:T(8,128)(2,1)S(1)} %reshape.49), channel_id=1, source_target_pairs={{0,8},{8,0},{16,24},{24,16},{32,40},{40,32},{48,56},{56,48},{64,72... | collective-permute-start | bytes 393224 | tf_op jit(solution)/shard_map/ppermute | solution.py:100
  120.3 0.0 copy-done.4
  120.3 0.1 slice.67
  120.4 0.1 copy.21
  120.5 0.2 convolution_bitcast_fusion
  120.7 0.5 collective-permute-done.3
  121.2 0.9 fusion
  (15 shorter events, 0.3 us)
Async XLA Ops:
  0.0 45.2 %copy-start = (bf16[1,512,1024]{2,1,0:T(8,128)(2,1)S(1)}, bf16[1,512,1024]{2,1,0:T(8,128)(2,1)}, u32[]{:S(2)}) copy-start(bf16[1,512,1024]{2,1,0:T(8,128)(2,1)} %param.10) | copy-start | bytes 3145732
  0.0 0.8 copy-start.6
  0.1 0.6 copy-start.9
  0.9 0.6 copy-start.3
  2.0 0.8 copy-start.5
  3.1 17.0 %collective-permute-start = (bf16[128,512]{1,0:T(8,128)(2,1)S(1)}, bf16[128,512]{1,0:T(8,128)(2,1)S(1)}, u32[]{:S(2)}, u32[]{:S(2)}) collective-permute-start(bf16[128,512]{1,0:T(8,128)(2,1)S(1)} %get-tuple-element.14), channel_id=1, source_target_pairs={{0,8},{8,0},{16,24},{24,16},{32,40},{40,32},{48,56},{56,48},{64,72... | collective-permute-start | bytes 393224 | tf_op jit(solution)/shard_map/ppermute | solution.py:63
  19.2 25.7 %copy-start.2 = (bf16[1,512,1024]{2,1,0:T(8,128)(2,1)S(1)}, bf16[1,512,1024]{2,1,0:T(8,128)(2,1)}, u32[]{:S(2)}) copy-start(bf16[1,512,1024]{2,1,0:T(8,128)(2,1)} %param.11) | copy-start | bytes 3145732
  21.1 23.6 %all-to-all-start = ((bf16[64,4,512]{2,1,0:T(4,128)(2,1)}), bf16[64,4,512]{2,1,0:T(4,128)(2,1)S(1)}, u32[]{:S(2)}, u32[]{:S(2)}) async-start(bf16[64,4,512]{2,1,0:T(4,128)(2,1)} %pad_maximum_fusion.2), calls=%async_computation | async-start | bytes 524288 | tf_op jit(solution)/shard_map/all_to_all | solution.py:45
  31.6 0.7 copy-start.11
  45.5 11.1 %collective-permute-start.1 = (bf16[128,2048]{1,0:T(8,128)(2,1)S(1)}, bf16[128,2048]{1,0:T(8,128)(2,1)S(1)}, u32[]{:S(2)}, u32[]{:S(2)}) collective-permute-start(bf16[128,2048]{1,0:T(8,128)(2,1)S(1)} %pad_maximum_fusion), channel_id=1, source_target_pairs={{0,1},{1,0},{2,3},{3,2},{4,5},{5,4},{6,7},{7,6},{9,10},{10,9},{11,... | collective-permute-start | bytes 1572872 | tf_op jit(solution)/shard_map/ppermute | solution.py:78
  70.9 17.5 %copy-start.1 = (bf16[1,1024,512]{2,1,0:T(8,128)(2,1)S(1)}, bf16[1,1024,512]{2,1,0:T(8,128)(2,1)}, u32[]{:S(2)}) copy-start(bf16[1,1024,512]{2,1,0:T(8,128)(2,1)} %param.12) | copy-start | bytes 3145732
  80.9 11.3 %collective-permute-start.2 = (bf16[128,1024]{1,0:T(8,128)(2,1)S(1)}, bf16[128,1024]{1,0:T(8,128)(2,1)S(1)}, u32[]{:S(2)}, u32[]{:S(2)}) collective-permute-start(bf16[128,1024]{1,0:T(8,128)(2,1)S(1)} %bitcast.39), channel_id=1, source_target_pairs={{0,1},{1,0},{2,3},{3,2},{4,5},{5,4},{6,7},{7,6},{9,10},{10,9},{11,... | collective-permute-start | bytes 786440 | tf_op jit(solution)/shard_map/ppermute | solution.py:93
  93.3 6.4 %copy-start.7 = (s32[32,4]{0,1:T(4,128)S(1)}, s32[32,4]{0,1:T(4,128)}, u32[]{:S(2)}) copy-start(s32[32,4]{0,1:T(4,128)} %param.8) | copy-start | bytes 1540
  93.3 6.4 %copy-start.8 = (f32[32,4]{0,1:T(4,128)S(1)}, f32[32,4]{0,1:T(4,128)}, u32[]{:S(2)}) copy-start(f32[32,4]{0,1:T(4,128)} %param.9) | copy-start | bytes 1540
  93.3 18.9 %all-to-all-start.3 = ((bf16[64,4,512]{2,1,0:T(4,128)(2,1)}), bf16[64,4,512]{2,1,0:T(4,128)(2,1)S(1)}, u32[]{:S(2)}, u32[]{:S(2)}) async-start(bf16[64,4,512]{2,1,0:T(4,128)(2,1)} %reshape.48), calls=%async_computation.3 | async-start | bytes 524288 | tf_op jit(solution)/shard_map/all_to_all | solution.py:45
  99.7 0.7 copy-start.10
  112.4 7.9 %copy-start.4 = (pred[128,32]{0,1:T(8,128)(4,1)S(1)}, pred[128,32]{0,1:T(8,128)(4,1)}, u32[]{:S(2)}) copy-start(pred[128,32]{0,1:T(8,128)(4,1)} %copy-done.3) | copy-start | bytes 12292
  112.5 8.8 %collective-permute-start.3 = (bf16[128,512]{1,0:T(8,128)(2,1)S(1)}, bf16[128,512]{1,0:T(8,128)(2,1)S(1)}, u32[]{:S(2)}, u32[]{:S(2)}) collective-permute-start(bf16[128,512]{1,0:T(8,128)(2,1)S(1)} %reshape.49), channel_id=1, source_target_pairs={{0,8},{8,0},{16,24},{24,16},{32,40},{40,32},{48,56},{56,48},{64,72... | collective-permute-start | bytes 393224 | tf_op jit(solution)/shard_map/ppermute | solution.py:100

commit v3 on v1

v3 whole, which is shorter than its diff:
```python
import jax
import jax.numpy as jnp
from jax import lax
from jax.sharding import PartitionSpec as P


CAP = 2
CORES = 2
BOTH = ("node", "local")
TEAMS = ((0, 2, 5, 7), (1, 3, 4, 6))
TEAM = (0, 1, 0, 1, 1, 0, 1, 0)


def body(tokens, node_ids, mix_weights, w_gate, w_up, w_down):
    row_count, feat_width = tokens.shape
    node_count = lax.axis_size("node")
    local_count = lax.axis_size("local")
    hidden = w_gate.shape[2]
    members = len(TEAMS[0])
    share = node_count // members

    nodes, places = range(node_count), range(local_count)

    def seat(node, label):
        return node * local_count + (label + node % CORES) % local_count

    def mate(place, core):
        return ((place - core) % local_count ^ 1) + core

    team_groups = [[seat(node, label) for label in team] for node in nodes for team in TEAMS]
    ring_groups = [[seat(node, label) for team in TEAMS for label in team] for node in nodes]
    pair_swap = [(seat(node, label), seat(node, label ^ 1)) for node in nodes for label in places]
    place = lax.axis_index("local")
    slot_of = [
        sum(jnp.where(place == (label + core) % local_count, team, 0) for label, team in enumerate(TEAM))
        for core in range(CORES)
    ]

    def exchange(array, axis, groups=None):
        return lax.all_to_all(
            array, axis, split_axis=0, concat_axis=0, tiled=True, axis_index_groups=groups
        )

    def dot(left, right):
        return jnp.dot(left, right, preferred_element_type=jnp.float32)

    tokens_pair = [
        lax.ppermute(tokens, "local", [(p, mate(p, core) % local_count) for p in places])
        for core in range(CORES)
    ]
    gate_pair = lax.ppermute(w_gate[0], BOTH, pair_swap)
    up_pair = lax.ppermute(w_up[0], BOTH, pair_swap)

    lines = jnp.arange(CAP * node_count, dtype=jnp.int32)[:, None]
    match = node_ids.T[:, None, :] == (lines // CAP)[None]
    hit = jnp.any(match, axis=0)
    weight = jnp.sum(jnp.where(match, mix_weights.T[:, None, :], 0.0), axis=0)
    earlier = jnp.arange(row_count)[:, None] < jnp.arange(row_count)[None, :]
    rank = dot(hit.astype(jnp.bfloat16), earlier.astype(jnp.bfloat16))
    combine = jnp.where(rank == (lines % CAP).astype(jnp.float32), weight, 0.0)
    core_line = lines // CAP % CORES
    slot = jnp.where(core_line == 0, slot_of[0], slot_of[1]).astype(jnp.float32)
    chosen = hit & (rank == slot)
    own_line = lines % CAP == 0
    dispatch = jnp.concatenate(
        [chosen & own_line] + [chosen & ~own_line & (core_line == core) for core in range(CORES)], axis=1
    )

    slices = jnp.concatenate([tokens] + tokens_pair, axis=0)
    outbound = dot(dispatch.astype(jnp.bfloat16), slices).astype(jnp.bfloat16)
    outbound, combine = lax.optimization_barrier((outbound, combine))
    inbound = exchange(outbound.reshape(node_count, CAP, feat_width), "node")
    mine, theirs = inbound[:, 0], inbound[:, 1]
    gate = dot(mine, w_gate[0]) + dot(theirs, gate_pair)
    up = dot(mine, w_up[0]) + dot(theirs, up_pair)
    sums = jnp.concatenate([gate.astype(jnp.bfloat16), up.astype(jnp.bfloat16)], axis=1)
    parts = exchange(sums.reshape(members, share, 2 * hidden), BOTH, team_groups)
    total = jnp.sum(parts.astype(jnp.float32), axis=0)
    active = (jax.nn.silu(total[:, :hidden]) * total[:, hidden:]).astype(jnp.bfloat16)

    copies = jnp.broadcast_to(active[None], (local_count, share, hidden))
    rows = exchange(copies, BOTH, ring_groups).reshape(CAP, node_count, hidden)
    result = jnp.stack([dot(rows[place], w_down[0]).astype(jnp.bfloat16) for place in range(CAP)], axis=1)
    returned = exchange(result, "node").reshape(CAP * node_count, feat_width)
    mixed = lax.dot_general(
        combine,
        returned.astype(jnp.float32),
        (((0,), (0,)), ((), ())),
        precision=lax.Precision.HIGHEST,
    )
    return mixed.astype(jnp.bfloat16)


def solution(mesh):
    return jax.shard_map(
        body,
        mesh=mesh,
        in_specs=(
            P("node", "local"),
            P("node", None),
            P("node", None),
            P("node", "local", None),
            P("node", "local", None),
            P("node", None, "local"),
        ),
        out_specs=P("node", "local"),
        check_vma=False,
    )
```

time: 122 us -> 134 us (1.098)
  starting transfers between devices: 10.7 us -> 39.7 us
  blocking collectives: 89.3 us -> 65.1 us
  waiting for transfers between devices: 13.9 us -> 19 us
  matrix products: 3.44 us -> 5.17 us
    all_to_all x3, blocking collectives: 89.3 us -> 65.1 us  [exchange(): lax.all_to_all(array, axis, split_axis=0, concat_axis=0, tiled=True, axis...]
    all_to_all x1, starting transfers between devices: 10.7 us -> 25.8 us  [exchange(): lax.all_to_all(array, axis, split_axis=0, concat_axis=0, tiled=True, axis...]
    ppermute x0 -> x4, starting transfers between devices: none -> 13.9 us  [the longest x2 7.36 us: body(): lax.ppermute(tokens, 'local', [(p, mate(p, core) % local_count) for p in...]
    ppermute x0 -> x4, waiting for transfers between devices: none -> 11.3 us  [the longest x1 9.59 us: body(): gate_pair = lax.ppermute(w_gate[0], BOTH, pair_swap)]
    all_to_all x1, waiting for transfers between devices: 13.9 us -> 7.7 us  [exchange(): lax.all_to_all(array, axis, split_axis=0, concat_axis=0, tiled=True, axis...]
    dot_general x5 -> x8, matrix products: 2.55 us -> 4.31 us  [dot(): return jnp.dot(left, right, preferred_element_type=jnp.float32)]
  transfers between devices with their start and end apart: 1 -> 5, of which waited for: 1 -> 4; matrix products, arithmetic and copies ran while one was open for 0% -> 3% of each run, Pallas kernels for 0% -> 0%
where the time goes in v3:
time: 134 us
  blocking collectives  65.1 us (49%)
  starting transfers between devices  39.7 us (30%)
  waiting for transfers between devices  19 us (14%)
  matrix products  5.17 us (4%)
  local copies, waits for them, and re-layouts  2.53 us (2%)
  other arithmetic  1.82 us (1%)
    all_to_all x3, blocking collectives, exchange(): lax.all_to_all(array, axis, split_axis=0, concat_axis=0, tiled=True, axis...  65.1 us
    all_to_all x1, starting transfers between devices, exchange(): lax.all_to_all(array, axis, split_axis=0, concat_axis=0, tiled=True, axis...  25.8 us
    ppermute x1, waiting for transfers between devices, body(): gate_pair = lax.ppermute(w_gate[0], BOTH, pair_swap)  9.59 us
    all_to_all x1, waiting for transfers between devices, exchange(): lax.all_to_all(array, axis, split_axis=0, concat_axis=0, tiled=True, axis...  7.7 us
    ppermute x2, starting transfers between devices, body(): lax.ppermute(tokens, 'local', [(p, mate(p, core) % local_count) for p in...  7.36 us
    dot_general x8, matrix products, dot(): return jnp.dot(left, right, preferred_element_type=jnp.float32)  4.31 us
    ppermute x1, starting transfers between devices, body(): gate_pair = lax.ppermute(w_gate[0], BOTH, pair_swap)  4.01 us
  transfers between devices with their start and end apart: 5, of which 4 were waited for; matrix products, arithmetic and copies ran while one was open for 3% of the time, Pallas kernels for 0%

profile of v3, /device:TPU:1, one launch (start us, length us, event | category | flops | bytes accessed | tf_op | source)
XLA Modules:
  0.0 133.7 jit_solution(15363533629763724871)
XLA Ops:
  0.0 0.0 copy-start
  0.0 0.0 copy-start.1
  0.0 5.4 %collective-permute-start.1 = (bf16[32,512]{1,0:T(8,128)(2,1)}, bf16[32,512]{1,0:T(8,128)(2,1)S(1)}, u32[]{:S(2)}, u32[]{:S(2)}) collective-permute-start(bf16[32,512]{1,0:T(8,128)(2,1)} %param.6), channel_id=1, source_target_pairs={{0,7},{1,2},{2,1},{3,4},{4,3},{5,6},{6,5},{7,0},{8,15},{9,10},{10,... | collective-permute-start | bytes 98312 | tf_op jit(solution)/shard_map/ppermute | solution.py:48
  5.5 1.9 %collective-permute-start = (bf16[32,512]{1,0:T(8,128)(2,1)}, bf16[32,512]{1,0:T(8,128)(2,1)S(1)}, u32[]{:S(2)}, u32[]{:S(2)}) collective-permute-start(bf16[32,512]{1,0:T(8,128)(2,1)} %param.6), channel_id=1, source_target_pairs={{0,1},{1,0},{2,3},{3,2},{4,5},{5,4},{6,7},{7,6},{8,9},{9,8},{10,11... | collective-permute-start | bytes 98312 | tf_op jit(solution)/shard_map/ppermute | solution.py:48
  7.5 0.8 compare_reduce_fusion
  8.3 0.8 fusion.6
  9.1 0.2 broadcast_and_fusion
  9.3 0.0 collective-permute-done.1
  9.3 1.0 collective-permute-done
  10.3 1.0 convolution_convert_fusion
  11.4 0.8 reshape.117
  12.1 25.8 %all-to-all-start = ((bf16[128,2,512]{2,1,0:T(2,128)(2,1)}), bf16[128,2,512]{2,1,0:T(2,128)(2,1)S(1)}, u32[]{:S(2)}, u32[]{:S(2)}) async-start(bf16[128,2,512]{2,1,0:T(2,128)(2,1)} %reshape.117), calls=%async_computation | async-start | bytes 524288 | tf_op jit(solution)/shard_map/all_to_all | solution.py:40
  38.0 0.0 copy-done.1
  38.0 2.5 %collective-permute-start.3 = (bf16[512,1024]{1,0:T(8,128)(2,1)S(1)}, bf16[512,1024]{1,0:T(8,128)(2,1)}, u32[]{:S(2)}, u32[]{:S(2)}) collective-permute-start(bf16[512,1024]{1,0:T(8,128)(2,1)S(1)} %bitcast.36), channel_id=1, source_target_pairs={{0,1},{1,0},{2,3},{3,2},{4,5},{5,4},{6,7},{7,6},{9,10},{10,9},{11,... | collective-permute-start | bytes 3145736 | tf_op jit(solution)/shard_map/ppermute | solution.py:52
  40.5 4.0 %collective-permute-start.2 = (bf16[512,1024]{1,0:T(8,128)(2,1)}, bf16[512,1024]{1,0:T(8,128)(2,1)S(1)}, u32[]{:S(2)}, u32[]{:S(2)}) collective-permute-start(bf16[512,1024]{1,0:T(8,128)(2,1)} %bitcast.37), channel_id=1, source_target_pairs={{0,1},{1,0},{2,3},{3,2},{4,5},{5,4},{6,7},{7,6},{9,10},{10,9},{11,... | collective-permute-start | bytes 3145736 | tf_op jit(solution)/shard_map/ppermute | solution.py:51
  44.5 7.7 %all-to-all-done = bf16[128,2,512]{2,1,0:T(2,128)(2,1)S(1)} async-done(((bf16[128,2,512]{2,1,0:T(2,128)(2,1)}), bf16[128,2,512]{2,1,0:T(2,128)(2,1)S(1)}, u32[]{:S(2)}, u32[]{:S(2)}) %all-to-all-start) | async-done | bytes 262176 | tf_op jit(solution)/shard_map/all_to_all | solution.py:40
  52.2 0.4 fusion.31
  52.6 0.0 copy-start.2
  52.6 0.3 fusion.18
  52.9 0.9 copy-done.2
  53.8 0.3 fusion.19
  54.1 0.7 collective-permute-done.3
  54.9 1.5 %fusion.1 = bf16[128,1024]{1,0:T(8,128)(2,1)S(1)} fusion(f32[128,1024]{1,0:T(8,128)S(1)} %fusion.18, bf16[512,1024]{1,0:T(8,128)(2,1)} %collective-permute-done.3, bf16[128,1,512]{2,1,0:T(2,128)(2,1)S(1)} %get-tuple-element.13), kind=kOutput, calls=%fused_computation.4 | convolution fusion | flops 134479872 | bytes 1966080 | tf_op jit(solution)/shard_map/dot_general | solution.py:45
  56.4 9.6 %collective-permute-done.2 = bf16[512,1024]{1,0:T(8,128)(2,1)S(1)} collective-permute-done((bf16[512,1024]{1,0:T(8,128)(2,1)}, bf16[512,1024]{1,0:T(8,128)(2,1)S(1)}, u32[]{:S(2)}, u32[]{:S(2)}) %collective-permute-start.2) | collective-permute-done | bytes 1048608 | tf_op jit(solution)/shard_map/ppermute | solution.py:51
  66.0 0.3 fusion
  66.4 17.7 %all_to_all.20 = bf16[4,32,2048]{2,1,0:T(8,128)(2,1)S(1)} all-to-all(bf16[4,32,2048]{2,1,0:T(8,128)(2,1)S(1)} %bitcast.35), channel_id=1, replica_groups={{0,2,5,7},{1,3,4,6},{9,11,14,8},{10,12,13,15},{16,18,21,23},{17,19,20,2..., dimensions={0} | all-to-all | bytes 1048576 | tf_op jit(solution)/shard_map/all_to_all | solution.py:40
  84.0 0.1 convert_reduce_fusion
  84.2 0.1 broadcast_in_dim.41
  84.2 17.6 %all_to_all.21 = bf16[8,32,1024]{2,1,0:T(8,128)(2,1)S(1)} all-to-all(bf16[8,32,1024]{2,1,0:T(8,128)(2,1)S(1)} %broadcast_in_dim.41), channel_id=1, replica_groups={{0,2,5,7,1,3,4,6},{9,11,14,8,10,12,13,15},{16,18,21,23,17,19,20,22},{25..., dimensions={0} | all-to-all | bytes 1048576 | tf_op jit(solution)/shard_map/all_to_all | solution.py:40
  101.8 0.0 copy-done
  101.8 0.3 fusion.3
  102.1 0.3 fusion.2
  102.5 0.3 copy.14
  102.8 29.9 %all_to_all.22 = bf16[128,2,512]{2,1,0:T(2,128)(2,1)S(1)} all-to-all(bf16[128,2,512]{2,1,0:T(2,128)(2,1)S(1)} %copy.14), channel_id=1, replica_groups=mesh['node'=128,'local'=8] {'node'}, dimensions={0} | all-to-all | bytes 524288 | tf_op jit(solution)/shard_map/all_to_all | solution.py:40
  132.7 0.1 reshape.119
  132.8 0.9 convolution_convert_fusion.3
  (12 shorter events, 0.2 us)
Async XLA Ops:
  0.0 101.8 %copy-start = (bf16[1,1024,512]{2,1,0:T(8,128)(2,1)S(1)}, bf16[1,1024,512]{2,1,0:T(8,128)(2,1)}, u32[]{:S(2)}) copy-start(bf16[1,1024,512]{2,1,0:T(8,128)(2,1)} %param.11) | copy-start | bytes 3145732
  0.0 38.0 %copy-start.1 = (bf16[1,512,1024]{2,1,0:T(8,128)(2,1)S(1)}, bf16[1,512,1024]{2,1,0:T(8,128)(2,1)}, u32[]{:S(2)}) copy-start(bf16[1,512,1024]{2,1,0:T(8,128)(2,1)} %param.10) | copy-start | bytes 3145732
  0.0 9.3 %collective-permute-start.1 = (bf16[32,512]{1,0:T(8,128)(2,1)}, bf16[32,512]{1,0:T(8,128)(2,1)S(1)}, u32[]{:S(2)}, u32[]{:S(2)}) collective-permute-start(bf16[32,512]{1,0:T(8,128)(2,1)} %param.6), channel_id=1, source_target_pairs={{0,7},{1,2},{2,1},{3,4},{4,3},{5,6},{6,5},{7,0},{8,15},{9,10},{10,... | collective-permute-start | bytes 98312 | tf_op jit(solution)/shard_map/ppermute | solution.py:48
  5.5 4.9 %collective-permute-start = (bf16[32,512]{1,0:T(8,128)(2,1)}, bf16[32,512]{1,0:T(8,128)(2,1)S(1)}, u32[]{:S(2)}, u32[]{:S(2)}) collective-permute-start(bf16[32,512]{1,0:T(8,128)(2,1)} %param.6), channel_id=1, source_target_pairs={{0,1},{1,0},{2,3},{3,2},{4,5},{5,4},{6,7},{7,6},{8,9},{9,8},{10,11... | collective-permute-start | bytes 98312 | tf_op jit(solution)/shard_map/ppermute | solution.py:48
  12.1 40.1 %all-to-all-start = ((bf16[128,2,512]{2,1,0:T(2,128)(2,1)}), bf16[128,2,512]{2,1,0:T(2,128)(2,1)S(1)}, u32[]{:S(2)}, u32[]{:S(2)}) async-start(bf16[128,2,512]{2,1,0:T(2,128)(2,1)} %reshape.117), calls=%async_computation | async-start | bytes 524288 | tf_op jit(solution)/shard_map/all_to_all | solution.py:40
  38.0 16.9 %collective-permute-start.3 = (bf16[512,1024]{1,0:T(8,128)(2,1)S(1)}, bf16[512,1024]{1,0:T(8,128)(2,1)}, u32[]{:S(2)}, u32[]{:S(2)}) collective-permute-start(bf16[512,1024]{1,0:T(8,128)(2,1)S(1)} %bitcast.36), channel_id=1, source_target_pairs={{0,1},{1,0},{2,3},{3,2},{4,5},{5,4},{6,7},{7,6},{9,10},{10,9},{11,... | collective-permute-start | bytes 3145736 | tf_op jit(solution)/shard_map/ppermute | solution.py:52
  40.5 25.5 %collective-permute-start.2 = (bf16[512,1024]{1,0:T(8,128)(2,1)}, bf16[512,1024]{1,0:T(8,128)(2,1)S(1)}, u32[]{:S(2)}, u32[]{:S(2)}) collective-permute-start(bf16[512,1024]{1,0:T(8,128)(2,1)} %bitcast.37), channel_id=1, source_target_pairs={{0,1},{1,0},{2,3},{3,2},{4,5},{5,4},{6,7},{7,6},{9,10},{10,9},{11,... | collective-permute-start | bytes 3145736 | tf_op jit(solution)/shard_map/ppermute | solution.py:51
  52.6 1.2 copy-start.2

commit v4 on v3

v4 whole, which is shorter than its diff:
```python
import jax
import jax.numpy as jnp
from jax import lax
from jax.experimental import pallas as pl
from jax.experimental.pallas import tpu as pltpu
from jax.sharding import PartitionSpec as P


CAP = 2
CORES = 2
BOTH = ("node", "local")
TEAMS = ((0, 2, 5, 7), (1, 3, 4, 6))
TEAM = (0, 1, 0, 1, 1, 0, 1, 0)


def dot(left, right):
    return jnp.dot(left, right, preferred_element_type=jnp.float32)


def one_hot_rows(rows, columns, place, transpose=False):
    line = lax.broadcasted_iota(jnp.int32, (rows, columns), 0)
    column = lax.broadcasted_iota(jnp.int32, (rows, columns), 1)
    same = line == column * CAP + place if transpose else column == line * CAP + place
    return same.astype(jnp.float32).astype(jnp.bfloat16)


def route_kernel(slot_ref, ids_ref, mix_ref, own_ref, first_ref, second_ref, out_ref, high_ref, low_ref):
    lines, row_count = high_ref.shape
    line = lax.broadcasted_iota(jnp.int32, (lines, row_count), 0)
    expert, part = line // CAP, line % CAP
    parity = expert % CORES
    hit = jnp.zeros((lines, row_count), jnp.float32)
    weight = jnp.zeros((lines, row_count), jnp.float32)
    for pick in range(ids_ref.shape[0]):
        match = ids_ref[pick : pick + 1, :] == expert
        hit = jnp.where(match, 1.0, hit)
        weight = jnp.where(match, mix_ref[pick : pick + 1, :], weight)
    before = lax.broadcasted_iota(jnp.int32, (row_count, row_count), 0)
    after = lax.broadcasted_iota(jnp.int32, (row_count, row_count), 1)
    earlier = jnp.where(before < after, 1.0, 0.0).astype(jnp.bfloat16)
    rank = dot(hit.astype(jnp.bfloat16), earlier)
    combine = jnp.where(rank == part.astype(jnp.float32), weight, 0.0)
    high = combine.astype(jnp.bfloat16)
    high_ref[...] = high
    low_ref[...] = (combine - high.astype(jnp.float32)).astype(jnp.bfloat16)
    slot = jnp.where(parity == 0, slot_ref[0], slot_ref[1]).astype(jnp.float32)
    chosen = jnp.where(rank == slot, hit, 0.0)
    total = dot(jnp.where(part == 0, chosen, 0.0).astype(jnp.bfloat16), own_ref[...])
    theirs = jnp.where(part == 1, chosen, 0.0)
    for core, ref in enumerate((first_ref, second_ref)):
        total = total + dot(jnp.where(parity == core, theirs, 0.0).astype(jnp.bfloat16), ref[...])
    out_ref[...] = total.astype(jnp.bfloat16)


def project_kernel(rows_ref, own_ref, pair_ref, out_ref):
    lines = rows_ref.shape[0]
    rows = rows_ref[...]
    mine = dot(one_hot_rows(lines // CAP, lines, 0), rows).astype(jnp.bfloat16)
    theirs = dot(one_hot_rows(lines // CAP, lines, 1), rows).astype(jnp.bfloat16)
    out_ref[...] = (dot(mine, own_ref[...]) + dot(theirs, pair_ref[...])).astype(jnp.bfloat16)


def down_kernel(rows_ref, w_ref, out_ref):
    half = rows_ref.shape[0] // CAP
    total = 0.0
    for place in range(CAP):
        result = dot(rows_ref[place * half : (place + 1) * half, :], w_ref[...]).astype(jnp.bfloat16)
        total = total + dot(one_hot_rows(CAP * half, half, place, True), result)
    out_ref[...] = total.astype(jnp.bfloat16)


def combine_kernel(high_ref, low_ref, rows_ref, out_ref):
    rows = rows_ref[...]
    total = 0.0
    for ref in (high_ref, low_ref):
        total = total + lax.dot_general(
            ref[...], rows, (((0,), (0,)), ((), ())), preferred_element_type=jnp.float32
        )
    out_ref[...] = total.astype(jnp.bfloat16)


def run(kernel, shapes, *operands, final=False):
    specs = [
        pl.BlockSpec(memory_space=pltpu.SMEM if array.ndim == 1 else pltpu.VMEM) for array in operands
    ]
    operands = [
        array if array.ndim == 1 else pltpu.with_memory_space_constraint(array, pltpu.VMEM)
        for array in operands
    ]
    outs = [
        jax.ShapeDtypeStruct(shape, jnp.bfloat16) if final else pltpu.VMEM(shape, jnp.bfloat16)
        for shape in shapes
    ]
    result = pl.pallas_call(
        kernel,
        in_specs=specs,
        out_specs=[pl.BlockSpec(memory_space=pltpu.VMEM)] * len(outs),
        out_shape=outs,
        compiler_params=pltpu.CompilerParams(vmem_limit_bytes=16 << 20),
    )(*operands)
    return result if len(outs) > 1 else result[0]


def body(tokens, node_ids, mix_weights, w_gate, w_up, w_down):
    row_count, feat_width = tokens.shape
    node_count = lax.axis_size("node")
    local_count = lax.axis_size("local")
    hidden = w_gate.shape[2]
    members = len(TEAMS[0])
    share = node_count // members

    nodes, places = range(node_count), range(local_count)

    def seat(node, label):
        return node * local_count + (label + node % CORES) % local_count

    def mate(place, core):
        return ((place - core) % local_count ^ 1) + core

    team_groups = [[seat(node, label) for label in team] for node in nodes for team in TEAMS]
    ring_groups = [[seat(node, label) for team in TEAMS for label in team] for node in nodes]
    pair_swap = [(seat(node, label), seat(node, label ^ 1)) for node in nodes for label in places]
    place = lax.axis_index("local")
    slot_of = [
        sum(jnp.where(place == (label + core) % local_count, team, 0) for label, team in enumerate(TEAM))
        for core in range(CORES)
    ]

    def exchange(array, axis, groups=None):
        return lax.all_to_all(
            array, axis, split_axis=0, concat_axis=0, tiled=True, axis_index_groups=groups
        )

    tokens_pair = [
        lax.ppermute(tokens, "local", [(p, mate(p, core) % local_count) for p in places])
        for core in range(CORES)
    ]
    w_own = jnp.concatenate([w_gate[0], w_up[0]], axis=1)
    w_pair = lax.ppermute(w_own, BOTH, pair_swap)

    lines = CAP * node_count
    outbound, high, low = run(
        route_kernel,
        [(lines, feat_width), (lines, row_count), (lines, row_count)],
        jnp.stack(slot_of).astype(jnp.int32),
        node_ids.T,
        mix_weights.T,
        tokens,
        *tokens_pair,
    )
    inbound = exchange(outbound.reshape(node_count, CAP, feat_width), "node")
    sums = run(
        project_kernel, [(node_count, 2 * hidden)], inbound.reshape(lines, feat_width), w_own, w_pair
    )
    parts = exchange(sums.reshape(members, share, 2 * hidden), BOTH, team_groups)
    total = jnp.sum(parts.astype(jnp.float32), axis=0)
    active = (jax.nn.silu(total[:, :hidden]) * total[:, hidden:]).astype(jnp.bfloat16)

    copies = jnp.broadcast_to(active[None], (local_count, share, hidden))
    rows = exchange(copies, BOTH, ring_groups).reshape(lines, hidden)
    result = run(down_kernel, [(lines, feat_width)], rows, w_down[0])
    returned = exchange(result.reshape(node_count, CAP, feat_width), "node").reshape(lines, feat_width)
    return run(combine_kernel, [(row_count, feat_width)], high, low, returned, final=True)


def solution(mesh):
    return jax.shard_map(
        body,
        mesh=mesh,
        in_specs=(
            P("node", "local"),
            P("node", None),
            P("node", None),
            P("node", "local", None),
            P("node", "local", None),
            P("node", None, "local"),
        ),
        out_specs=P("node", "local"),
        check_vma=False,
    )
```

time: 134 us -> 135 us (level)
  blocking collectives: 65.1 us -> 97.4 us
  starting transfers between devices: 39.7 us -> 11.4 us
  matrix products: 5.17 us -> 0 us
  Pallas kernels: 0 us -> 5.06 us
  local copies, waits for them, and re-layouts: 2.53 us -> 0.48 us
    all_to_all x3 -> x4, blocking collectives: 65.1 us -> 97.4 us  [exchange(): lax.all_to_all(array, axis, split_axis=0, concat_axis=0, tiled=True, axis...]
    all_to_all x1 -> x0, starting transfers between devices: 25.8 us -> none  [exchange(): lax.all_to_all(array, axis, split_axis=0, concat_axis=0, tiled=True, axis...]
    ppermute x2, waiting for transfers between devices: 0.98 us -> 18.3 us  [body(): lax.ppermute(tokens, 'local', [(p, mate(p, core) % local_count) for p in...]
    ppermute x2 -> x1, waiting for transfers between devices: 10.3 us -> 0.01 us  [body(): w_pair = lax.ppermute(w_own, BOTH, pair_swap)]
    all_to_all x1 -> x0, waiting for transfers between devices: 7.7 us -> none  [exchange(): lax.all_to_all(array, axis, split_axis=0, concat_axis=0, tiled=True, axis...]
    dot_general x9 -> x0, matrix products: 5.17 us -> none  [the longest x8 4.31 us: dot(): return jnp.dot(left, right, preferred_element_type=jnp.float32)]
    pallas_call x0 -> x4, Pallas kernels: none -> 5.06 us  [run(): pl.pallas_call(kernel, in_specs=specs, out_specs=[pl.BlockSpec(memory_spa...]
    concatenate x1, other arithmetic: 0.04 us -> 1.74 us  [body(): w_own = jnp.concatenate([w_gate[0], w_up[0]], axis=1)]
  transfers between devices with their start and end apart: 5 -> 3, of which waited for: 4 -> 1; matrix products, arithmetic and copies ran while one was open for 3% -> 0% of each run, Pallas kernels for 0% -> 1%
where the time goes in v4:
time: 135 us
  blocking collectives  97.4 us (72%)
  waiting for transfers between devices  18.3 us (14%)
  starting transfers between devices  11.4 us (8%)
  Pallas kernels  5.06 us (4%)
  other arithmetic  1.94 us (1%)
    all_to_all x4, blocking collectives, exchange(): lax.all_to_all(array, axis, split_axis=0, concat_axis=0, tiled=True, axis...  97.4 us
    ppermute x2, waiting for transfers between devices, body(): lax.ppermute(tokens, 'local', [(p, mate(p, core) % local_count) for p in...  18.3 us
    ppermute x2, starting transfers between devices, body(): lax.ppermute(tokens, 'local', [(p, mate(p, core) % local_count) for p in...  6.12 us
    ppermute x1, starting transfers between devices, body(): w_pair = lax.ppermute(w_own, BOTH, pair_swap)  5.32 us
    pallas_call x4, Pallas kernels, run(): pl.pallas_call(kernel, in_specs=specs, out_specs=[pl.BlockSpec(memory_spa...  5.06 us
  transfers between devices with their start and end apart: 3, of which 1 were waited for; matrix products, arithmetic and copies ran while one was open for 0% of the time, Pallas kernels for 1%

profile of v4, /device:TPU:1, one launch (start us, length us, event | category | flops | bytes accessed | tf_op | source)
XLA Modules:
  0.0 134.7 jit_solution(11117661643635515774)
XLA Ops:
  0.0 0.0 copy-start.1
  0.0 0.0 copy-start.2
  0.0 0.0 copy-start.3
  0.0 1.7 %pad_maximum_fusion.own_ref = bf16[512,2048]{1,0:T(8,128)(2,1)S(1)} fusion(bf16[512,1024]{1,0:T(8,128)(2,1)} %bitcast.14, bf16[512,1024]{1,0:T(8,128)(2,1)} %bitcast.15), kind=kLoop, calls=%fused_computation | loop fusion | flops 4194304 | bytes 4194304 | tf_op jit(solution)/shard_map/concatenate | solution.py:138
  1.8 5.3 %collective-permute-start.2 = (bf16[512,2048]{1,0:T(8,128)(2,1)S(1)}, bf16[512,2048]{1,0:T(8,128)(2,1)}, u32[]{:S(2)}, u32[]{:S(2)}) collective-permute-start(bf16[512,2048]{1,0:T(8,128)(2,1)S(1)} %pad_maximum_fusion.own_ref), channel_id=1, source_target_pairs={{0,1},{1,0},{2,3},{3,2},{4,5},{5,4},{6,7},{7,6},{9,10},{10,9},{11,... | collective-permute-start | bytes 6291464 | tf_op jit(solution)/shard_map/ppermute | solution.py:139
  7.1 0.0 copy-done.1
  7.1 1.9 %collective-permute-start = (bf16[32,512]{1,0:T(8,128)(2,1)S(1)}, bf16[32,512]{1,0:T(8,128)(2,1)S(1)}, u32[]{:S(2)}, u32[]{:S(2)}) collective-permute-start(bf16[32,512]{1,0:T(8,128)(2,1)S(1)} %copy-done.1), channel_id=1, source_target_pairs={{0,1},{1,0},{2,3},{3,2},{4,5},{5,4},{6,7},{7,6},{8,9},{9,8},{10,11... | collective-permute-start | bytes 98312 | tf_op jit(solution)/shard_map/ppermute | solution.py:135
  9.0 4.2 %collective-permute-start.1 = (bf16[32,512]{1,0:T(8,128)(2,1)S(1)}, bf16[32,512]{1,0:T(8,128)(2,1)S(1)}, u32[]{:S(2)}, u32[]{:S(2)}) collective-permute-start(bf16[32,512]{1,0:T(8,128)(2,1)S(1)} %copy-done.1), channel_id=1, source_target_pairs={{0,7},{1,2},{2,1},{3,4},{4,3},{5,6},{6,5},{7,0},{8,15},{9,10},{10,... | collective-permute-start | bytes 98312 | tf_op jit(solution)/shard_map/ppermute | solution.py:135
  13.3 0.1 pad_add_fusion.slot_ref
  13.3 0.0 collective-permute-done.first_ref
  13.3 18.3 %collective-permute-done.1.second_ref = bf16[32,512]{1,0:T(8,128)(2,1)S(1)} collective-permute-done((bf16[32,512]{1,0:T(8,128)(2,1)S(1)}, bf16[32,512]{1,0:T(8,128)(2,1)S(1)}, u32[]{:S(2)}, u32[]{:S(2)}) %collective-permute-start.1) | collective-permute-done | bytes 32800 | tf_op jit(solution)/shard_map/ppermute | solution.py:135
  31.6 0.0 copy-done.2
  31.6 0.0 copy-done.3
  31.6 1.0 shard_map.64
  32.6 0.1 reshape.19
  32.8 38.1 %all_to_all.20 = bf16[128,2,512]{2,1,0:T(2,128)(2,1)S(1)} all-to-all(bf16[128,2,512]{2,1,0:T(2,128)(2,1)S(1)} %reshape.19), channel_id=1, replica_groups=mesh['node'=128,'local'=8] {'node'}, dimensions={0} | all-to-all | bytes 524288 | tf_op jit(solution)/shard_map/all_to_all | solution.py:130
  70.9 0.1 reshape.20.rows_ref
  71.0 0.0 collective-permute-done.2.pair_ref
  71.0 2.5 %shard_map.65 = bf16[128,2048]{1,0:T(8,128)(2,1)S(1)} custom-call(bf16[256,512]{1,0:T(8,128)(2,1)S(1)} %reshape.20.rows_ref, bf16[512,2048]{1,0:T(8,128)(2,1)S(1)} %pad_maximum_fusion.own_ref, bf16[512,2048]{1,0:T(8,128)(2,1)} %collective-permute-done.2.pair_ref), custom_call_target="tpu_custom_call" | custom-call | tf_op jit(solution)/shard_map/pallas_call | solution.py:94
  73.5 0.0 copy-start
  73.5 15.7 %all_to_all.21 = bf16[4,32,2048]{2,1,0:T(8,128)(2,1)S(1)} all-to-all(bf16[4,32,2048]{2,1,0:T(8,128)(2,1)S(1)} %bitcast.9), channel_id=1, replica_groups={{0,2,5,7},{1,3,4,6},{9,11,14,8},{10,12,13,15},{16,18,21,23},{17,19,20,2..., dimensions={0} | all-to-all | bytes 1048576 | tf_op jit(solution)/shard_map/all_to_all | solution.py:130
  89.2 0.1 convert_reduce_fusion
  89.4 0.1 broadcast_in_dim.2
  89.4 21.0 %all_to_all.22 = bf16[8,32,1024]{2,1,0:T(8,128)(2,1)S(1)} all-to-all(bf16[8,32,1024]{2,1,0:T(8,128)(2,1)S(1)} %broadcast_in_dim.2), channel_id=1, replica_groups={{0,2,5,7,1,3,4,6},{9,11,14,8,10,12,13,15},{16,18,21,23,17,19,20,22},{25..., dimensions={0} | all-to-all | bytes 1048576 | tf_op jit(solution)/shard_map/all_to_all | solution.py:130
  110.4 0.0 copy-done
  110.4 0.7 shard_map.66
  111.2 0.1 reshape.23
  111.3 22.5 %all_to_all.23 = bf16[128,2,512]{2,1,0:T(2,128)(2,1)S(1)} all-to-all(bf16[128,2,512]{2,1,0:T(2,128)(2,1)S(1)} %reshape.23), channel_id=1, replica_groups=mesh['node'=128,'local'=8] {'node'}, dimensions={0} | all-to-all | bytes 524288 | tf_op jit(solution)/shard_map/all_to_all | solution.py:130
  133.8 0.1 reshape.24.rows_ref
  133.9 0.8 shard_map.67
  (1 shorter events, 0.0 us)
Async XLA Ops:
  0.0 7.1 %copy-start.1 = (bf16[32,512]{1,0:T(8,128)(2,1)S(1)}, bf16[32,512]{1,0:T(8,128)(2,1)}, u32[]{:S(2)}) copy-start(bf16[32,512]{1,0:T(8,128)(2,1)} %own_ref.1) | copy-start | bytes 98308
  0.0 31.6 %copy-start.2 = (s32[32,4]{0,1:T(4,128)S(1)}, s32[32,4]{0,1:T(4,128)}, u32[]{:S(2)}) copy-start(s32[32,4]{0,1:T(4,128)} %param.7) | copy-start | bytes 1540
  0.0 31.6 %copy-start.3 = (f32[32,4]{0,1:T(4,128)S(1)}, f32[32,4]{0,1:T(4,128)}, u32[]{:S(2)}) copy-start(f32[32,4]{0,1:T(4,128)} %param.8) | copy-start | bytes 1540
  1.8 69.2 %collective-permute-start.2 = (bf16[512,2048]{1,0:T(8,128)(2,1)S(1)}, bf16[512,2048]{1,0:T(8,128)(2,1)}, u32[]{:S(2)}, u32[]{:S(2)}) collective-permute-start(bf16[512,2048]{1,0:T(8,128)(2,1)S(1)} %pad_maximum_fusion.own_ref), channel_id=1, source_target_pairs={{0,1},{1,0},{2,3},{3,2},{4,5},{5,4},{6,7},{7,6},{9,10},{10,9},{11,... | collective-permute-start | bytes 6291464 | tf_op jit(solution)/shard_map/ppermute | solution.py:139
  7.1 6.3 %collective-permute-start = (bf16[32,512]{1,0:T(8,128)(2,1)S(1)}, bf16[32,512]{1,0:T(8,128)(2,1)S(1)}, u32[]{:S(2)}, u32[]{:S(2)}) collective-permute-start(bf16[32,512]{1,0:T(8,128)(2,1)S(1)} %copy-done.1), channel_id=1, source_target_pairs={{0,1},{1,0},{2,3},{3,2},{4,5},{5,4},{6,7},{7,6},{8,9},{9,8},{10,11... | collective-permute-start | bytes 98312 | tf_op jit(solution)/shard_map/ppermute | solution.py:135
  9.0 22.6 %collective-permute-start.1 = (bf16[32,512]{1,0:T(8,128)(2,1)S(1)}, bf16[32,512]{1,0:T(8,128)(2,1)S(1)}, u32[]{:S(2)}, u32[]{:S(2)}) collective-permute-start(bf16[32,512]{1,0:T(8,128)(2,1)S(1)} %copy-done.1), channel_id=1, source_target_pairs={{0,7},{1,2},{2,1},{3,4},{4,3},{5,6},{6,5},{7,0},{8,15},{9,10},{10,... | collective-permute-start | bytes 98312 | tf_op jit(solution)/shard_map/ppermute | solution.py:135
  73.5 36.9 %copy-start = (bf16[1,1024,512]{2,1,0:T(8,128)(2,1)S(1)}, bf16[1,1024,512]{2,1,0:T(8,128)(2,1)}, u32[]{:S(2)}) copy-start(bf16[1,1024,512]{2,1,0:T(8,128)(2,1)} %param.11) | copy-start | bytes 3145732

commit v5 on v4

--- a/solution.py
+++ b/solution.py
@@ -24,7 +24,26 @@
     return same.astype(jnp.float32).astype(jnp.bfloat16)
 
 
-def route_kernel(slot_ref, ids_ref, mix_ref, own_ref, first_ref, second_ref, out_ref, high_ref, low_ref):
+def prepare_kernel(
+    meta_ref, ids_hbm, mix_hbm, gate_ref, up_ref,
+    joined_ref, own_ref, first_ref, second_ref, high_ref, low_ref,
+    ids_ref, mix_ref, sems,
+):
+    hidden = gate_ref.shape[1]
+    tables = [
+        pltpu.make_async_copy(source, target, sems.at[2 + index])
+        for index, (source, target) in enumerate(((ids_hbm, ids_ref), (mix_hbm, mix_ref)))
+    ]
+    for table in tables:
+        table.start()
+    joins = [
+        pltpu.make_async_copy(ref, joined_ref.at[:, pl.ds(index * hidden, hidden)], sems.at[index])
+        for index, ref in enumerate((gate_ref, up_ref))
+    ]
+    for join in joins:
+        join.start()
+    for table in tables:
+        table.wait()
     lines, row_count = high_ref.shape
     line = lax.broadcasted_iota(jnp.int32, (lines, row_count), 0)
     expert, part = line // CAP, line % CAP
@@ -43,30 +62,48 @@
     high = combine.astype(jnp.bfloat16)
     high_ref[...] = high
     low_ref[...] = (combine - high.astype(jnp.float32)).astype(jnp.bfloat16)
-    slot = jnp.where(parity == 0, slot_ref[0], slot_ref[1]).astype(jnp.float32)
+    slot = jnp.where(parity == 0, meta_ref[0], meta_ref[1]).astype(jnp.float32)
     chosen = jnp.where(rank == slot, hit, 0.0)
-    total = dot(jnp.where(part == 0, chosen, 0.0).astype(jnp.bfloat16), own_ref[...])
+    own_ref[...] = jnp.where(part == 0, chosen, 0.0).astype(jnp.bfloat16)
     theirs = jnp.where(part == 1, chosen, 0.0)
     for core, ref in enumerate((first_ref, second_ref)):
-        total = total + dot(jnp.where(parity == core, theirs, 0.0).astype(jnp.bfloat16), ref[...])
+        ref[...] = jnp.where(parity == core, theirs, 0.0).astype(jnp.bfloat16)
+    for join in joins:
+        join.wait()
+
+
+def gather_kernel(*refs):
+    out_ref = refs[-1]
+    picks, slices = refs[: len(refs) // 2], refs[len(refs) // 2 : -1]
+    total = sum(dot(pick[...], rows[...]) for pick, rows in zip(picks, slices))
     out_ref[...] = total.astype(jnp.bfloat16)
 
 
-def project_kernel(rows_ref, own_ref, pair_ref, out_ref):
+def project_kernel(rows_ref, own_ref, pair_ref, out_ref, total_ref, pair_buf, sem):
+    copy = pltpu.make_async_copy(pair_ref, pair_buf, sem)
+    copy.start()
     lines = rows_ref.shape[0]
     rows = rows_ref[...]
     mine = dot(one_hot_rows(lines // CAP, lines, 0), rows).astype(jnp.bfloat16)
     theirs = dot(one_hot_rows(lines // CAP, lines, 1), rows).astype(jnp.bfloat16)
-    out_ref[...] = (dot(mine, own_ref[...]) + dot(theirs, pair_ref[...])).astype(jnp.bfloat16)
-
-
-def down_kernel(rows_ref, w_ref, out_ref):
-    half = rows_ref.shape[0] // CAP
-    total = 0.0
-    for place in range(CAP):
-        result = dot(rows_ref[place * half : (place + 1) * half, :], w_ref[...]).astype(jnp.bfloat16)
-        total = total + dot(one_hot_rows(CAP * half, half, place, True), result)
-    out_ref[...] = total.astype(jnp.bfloat16)
+    total_ref[...] = dot(mine, own_ref[...])
+    copy.wait()
+    out_ref[...] = (total_ref[...] + dot(theirs, pair_buf[...])).astype(jnp.bfloat16)
+
+
+def down_kernel(meta_ref, rows_ref, w_ref, out_ref, result_ref):
+    lines = rows_ref.shape[0]
+    ring = len(TEAM)
+    share = lines // ring
+    core = meta_ref[2]
+    result_ref[...] = dot(rows_ref[...], w_ref[...]).astype(jnp.bfloat16)
+    for member in range(len(TEAMS[0])):
+        total = 0.0
+        for place, team in enumerate(TEAMS):
+            seat = lax.rem(team[member] + core, ring)
+            block = result_ref[pl.ds(pl.multiple_of(seat * share, share), share), :]
+            total = total + dot(one_hot_rows(CAP * share, share, place, True), block)
+        out_ref[member * CAP * share : (member + 1) * CAP * share, :] = total.astype(jnp.bfloat16)
 
 
 def combine_kernel(high_ref, low_ref, rows_ref, out_ref):
@@ -79,14 +116,18 @@
     out_ref[...] = total.astype(jnp.bfloat16)
 
 
-def run(kernel, shapes, *operands, final=False):
-    specs = [
-        pl.BlockSpec(memory_space=pltpu.SMEM if array.ndim == 1 else pltpu.VMEM) for array in operands
-    ]
-    operands = [
-        array if array.ndim == 1 else pltpu.with_memory_space_constraint(array, pltpu.VMEM)
-        for array in operands
-    ]
+def run(kernel, shapes, *operands, hbm=(), scratch=(), final=False):
+    specs, placed = [], []
+    for index, array in enumerate(operands):
+        if array.ndim == 1:
+            specs.append(pl.BlockSpec(memory_space=pltpu.SMEM))
+        elif index in hbm:
+            specs.append(pl.BlockSpec(memory_space=pltpu.HBM))
+            array = pltpu.with_memory_space_constraint(array, pltpu.HBM)
+        else:
+            specs.append(pl.BlockSpec(memory_space=pltpu.VMEM))
+            array = pltpu.with_memory_space_constraint(array, pltpu.VMEM)
+        placed.append(array)
     outs = [
         jax.ShapeDtypeStruct(shape, jnp.bfloat16) if final else pltpu.VMEM(shape, jnp.bfloat16)
         for shape in shapes
@@ -96,8 +137,9 @@
         in_specs=specs,
         out_specs=[pl.BlockSpec(memory_space=pltpu.VMEM)] * len(outs),
         out_shape=outs,
+        scratch_shapes=list(scratch),
         compiler_params=pltpu.CompilerParams(vmem_limit_bytes=16 << 20),
-    )(*operands)
+    )(*placed)
     return result if len(outs) > 1 else result[0]
 
 
@@ -118,7 +160,6 @@
         return ((place - core) % local_count ^ 1) + core
 
     team_groups = [[seat(node, label) for label in team] for node in nodes for team in TEAMS]
-    ring_groups = [[seat(node, label) for team in TEAMS for label in team] for node in nodes]
     pair_swap = [(seat(node, label), seat(node, label ^ 1)) for node in nodes for label in places]
     place = lax.axis_index("local")
     slot_of = [
@@ -135,30 +176,55 @@
         lax.ppermute(tokens, "local", [(p, mate(p, core) % local_count) for p in places])
         for core in range(CORES)
     ]
-    w_own = jnp.concatenate([w_gate[0], w_up[0]], axis=1)
-    w_pair = lax.ppermute(w_own, BOTH, pair_swap)
-
     lines = CAP * node_count
-    outbound, high, low = run(
-        route_kernel,
-        [(lines, feat_width), (lines, row_count), (lines, row_count)],
-        jnp.stack(slot_of).astype(jnp.int32),
+    core = lax.axis_index("node") % CORES
+    meta = jnp.stack(slot_of + [core]).astype(jnp.int32)
+    w_own, *tables = run(
+        prepare_kernel,
+        [(feat_width, 2 * hidden)] + [(lines, row_count)] * 5,
+        meta,
         node_ids.T,
         mix_weights.T,
-        tokens,
-        *tokens_pair,
-    )
+        w_gate[0],
+        w_up[0],
+        hbm=(1, 2, 3, 4),
+        scratch=[
+            pltpu.VMEM(node_ids.shape[::-1], jnp.int32),
+            pltpu.VMEM(mix_weights.shape[::-1], jnp.float32),
+            pltpu.SemaphoreType.DMA((4,)),
+        ],
+    )
+    picks, (high, low) = tables[:3], tables[3:]
+    w_pair = lax.ppermute(w_own, BOTH, pair_swap)
+    outbound = run(gather_kernel, [(lines, feat_width)], *picks, tokens, *tokens_pair)
     inbound = exchange(outbound.reshape(node_count, CAP, feat_width), "node")
     sums = run(
-        project_kernel, [(node_count, 2 * hidden)], inbound.reshape(lines, feat_width), w_own, w_pair
+        project_kernel,
+        [(node_count, 2 * hidden)],
+        inbound.reshape(lines, feat_width),
+        w_own,
+        w_pair,
+        hbm=(2,),
+        scratch=[
+            pltpu.VMEM((node_count, 2 * hidden), jnp.float32),
+            pltpu.VMEM((feat_width, 2 * hidden), jnp.bfloat16),
+            pltpu.SemaphoreType.DMA,
+        ],
     )
     parts = exchange(sums.reshape(members, share, 2 * hidden), BOTH, team_groups)
     total = jnp.sum(parts.astype(jnp.float32), axis=0)
     active = (jax.nn.silu(total[:, :hidden]) * total[:, hidden:]).astype(jnp.bfloat16)
 
     copies = jnp.broadcast_to(active[None], (local_count, share, hidden))
-    rows = exchange(copies, BOTH, ring_groups).reshape(lines, hidden)
-    result = run(down_kernel, [(lines, feat_width)], rows, w_down[0])
+    rows = exchange(copies, "local").reshape(lines, hidden)
+    result = run(
+        down_kernel,
+        [(lines, feat_width)],
+        meta,
+        rows,
+        w_down[0],
+        scratch=[pltpu.VMEM((lines, feat_width), jnp.bfloat16)],
+    )
     returned = exchange(result.reshape(node_count, CAP, feat_width), "node").reshape(lines, feat_width)
     return run(combine_kernel, [(row_count, feat_width)], high, low, returned, final=True)
 

time: 135 us -> 137 us (1.015)
  blocking collectives: 97.4 us -> 99.8 us
  other arithmetic: 1.94 us -> 0.2 us
  Pallas kernels: 5.06 us -> 6.62 us
    all_to_all x4, blocking collectives: 97.4 us -> 99.8 us  [exchange(): lax.all_to_all(array, axis, split_axis=0, concat_axis=0, tiled=True, axis...]
    concatenate x1 -> x0, other arithmetic: 1.74 us -> none  [body(): w_own = jnp.concatenate([w_gate[0], w_up[0]], axis=1)]
    pallas_call x4 -> x5, Pallas kernels: 5.06 us -> 6.62 us  [run(): pl.pallas_call(kernel, in_specs=specs, out_specs=[pl.BlockSpec(memory_spa...]
  transfers between devices with their start and end apart: 3 -> 3, of which waited for: 1 -> 1; matrix products, arithmetic and copies ran while one was open for 0% -> 0% of each run, Pallas kernels for 1% -> 0%
where the time goes in v5:
time: 137 us
  blocking collectives  99.8 us (73%)
  waiting for transfers between devices  18.3 us (13%)
  starting transfers between devices  11.4 us (8%)
  Pallas kernels  6.62 us (5%)
    all_to_all x4, blocking collectives, exchange(): lax.all_to_all(array, axis, split_axis=0, concat_axis=0, tiled=True, axis...  99.8 us
    ppermute x2, waiting for transfers between devices, body(): lax.ppermute(tokens, 'local', [(p, mate(p, core) % local_count) for p in...  18.3 us
    pallas_call x5, Pallas kernels, run(): pl.pallas_call(kernel, in_specs=specs, out_specs=[pl.BlockSpec(memory_spa...  6.62 us
    ppermute x2, starting transfers between devices, body(): lax.ppermute(tokens, 'local', [(p, mate(p, core) % local_count) for p in...  6.12 us
    ppermute x1, starting transfers between devices, body(): w_pair = lax.ppermute(w_own, BOTH, pair_swap)  5.32 us
  transfers between devices with their start and end apart: 3, of which 1 were waited for; matrix products, arithmetic and copies ran while one was open for 0% of the time, Pallas kernels for 0%

profile of v5, /device:TPU:1, one launch (start us, length us, event | category | flops | bytes accessed | tf_op | source)
XLA Modules:
  0.0 137.0 jit_solution(13570170301334619077)
XLA Ops:
  0.0 0.0 copy-start.1
  0.0 0.1 pad_add_fusion.meta_ref
  0.1 2.1 %shard_map.64 = (bf16[512,2048]{1,0:T(8,128)(2,1)S(1)}, bf16[256,32]{1,0:T(8,128)(2,1)S(1)}, bf16[256,32]{1,0:T(8,128)(2,1)S(1)}, bf16[256,32]{1,0:T(8,128)(2,1)...) custom-call(s32[3]{0:T(128)S(1)} %pad_add_fusion.meta_ref, s32[4,32]{1,0:T(4,128)} %bitcast.15, ...), custom_call_target="tpu_custom_call" | custom-call | tf_op jit(solution)/shard_map/pallas_call | solution.py:135
  2.2 5.3 %collective-permute-start.2 = (bf16[512,2048]{1,0:T(8,128)(2,1)S(1)}, bf16[512,2048]{1,0:T(8,128)(2,1)}, u32[]{:S(2)}, u32[]{:S(2)}) collective-permute-start(bf16[512,2048]{1,0:T(8,128)(2,1)S(1)} %get-tuple-element.16.own_ref), channel_id=1, source_target_pairs={{0,1},{1,0},{2,3},{3,2},{4,5},{5,4},{6,7},{7,6},{9,10},{10,9},{11,... | collective-permute-start | bytes 6291464 | tf_op jit(solution)/shard_map/ppermute | solution.py:198
  7.6 0.0 copy-done.1
  7.6 1.9 %collective-permute-start = (bf16[32,512]{1,0:T(8,128)(2,1)S(1)}, bf16[32,512]{1,0:T(8,128)(2,1)S(1)}, u32[]{:S(2)}, u32[]{:S(2)}) collective-permute-start(bf16[32,512]{1,0:T(8,128)(2,1)S(1)} %copy-done.1), channel_id=1, source_target_pairs={{0,1},{1,0},{2,3},{3,2},{4,5},{5,4},{6,7},{7,6},{8,9},{9,8},{10,11... | collective-permute-start | bytes 98312 | tf_op jit(solution)/shard_map/ppermute | solution.py:176
  9.5 4.2 %collective-permute-start.1 = (bf16[32,512]{1,0:T(8,128)(2,1)S(1)}, bf16[32,512]{1,0:T(8,128)(2,1)S(1)}, u32[]{:S(2)}, u32[]{:S(2)}) collective-permute-start(bf16[32,512]{1,0:T(8,128)(2,1)S(1)} %copy-done.1), channel_id=1, source_target_pairs={{0,7},{1,2},{2,1},{3,4},{4,3},{5,6},{6,5},{7,0},{8,15},{9,10},{10,... | collective-permute-start | bytes 98312 | tf_op jit(solution)/shard_map/ppermute | solution.py:176
  13.7 0.0 collective-permute-done.refs_4_
  13.7 18.3 %collective-permute-done.1.refs_5_ = bf16[32,512]{1,0:T(8,128)(2,1)S(1)} collective-permute-done((bf16[32,512]{1,0:T(8,128)(2,1)S(1)}, bf16[32,512]{1,0:T(8,128)(2,1)S(1)}, u32[]{:S(2)}, u32[]{:S(2)}) %collective-permute-start.1) | collective-permute-done | bytes 32800 | tf_op jit(solution)/shard_map/ppermute | solution.py:176
  32.0 0.3 shard_map.65
  32.4 0.1 reshape.19
  32.5 38.2 %all_to_all.20 = bf16[128,2,512]{2,1,0:T(2,128)(2,1)S(1)} all-to-all(bf16[128,2,512]{2,1,0:T(2,128)(2,1)S(1)} %reshape.19), channel_id=1, replica_groups=mesh['node'=128,'local'=8] {'node'}, dimensions={0} | all-to-all | bytes 524288 | tf_op jit(solution)/shard_map/all_to_all | solution.py:171
  70.7 0.1 reshape.20.rows_ref
  70.8 0.0 collective-permute-done.2.pair_ref
  70.8 2.1 %shard_map.66 = bf16[128,2048]{1,0:T(8,128)(2,1)S(1)} custom-call(bf16[256,512]{1,0:T(8,128)(2,1)S(1)} %reshape.20.rows_ref, bf16[512,2048]{1,0:T(8,128)(2,1)S(1)} %get-tuple-element.16.own_ref, bf16[512,2048]{1,0:T(8,128)(2,1)} %collective-permute-done.2.pair_ref), custom_call_target="tpu_custom_call" | custom-call | tf_op jit(solution)/shard_map/pallas_call | solution.py:135
  72.8 0.0 copy-start
  72.8 15.7 %all_to_all.21 = bf16[4,32,2048]{2,1,0:T(8,128)(2,1)S(1)} all-to-all(bf16[4,32,2048]{2,1,0:T(8,128)(2,1)S(1)} %bitcast.10), channel_id=1, replica_groups={{0,2,5,7},{1,3,4,6},{9,11,14,8},{10,12,13,15},{16,18,21,23},{17,19,20,2..., dimensions={0} | all-to-all | bytes 1048576 | tf_op jit(solution)/shard_map/all_to_all | solution.py:171
  88.5 0.1 convert_reduce_fusion
  88.7 0.1 broadcast_in_dim.2
  88.7 23.7 %all_to_all.22 = bf16[8,32,1024]{2,1,0:T(8,128)(2,1)S(1)} all-to-all(bf16[8,32,1024]{2,1,0:T(8,128)(2,1)S(1)} %broadcast_in_dim.2), channel_id=1, replica_groups=mesh['node'=128,'local'=8] {'local'}, dimensions={0} | all-to-all | bytes 1048576 | tf_op jit(solution)/shard_map/all_to_all | solution.py:171
  112.4 0.0 copy-done
  112.4 1.2 shard_map.67
  113.7 0.1 reshape.23
  113.8 22.3 %all_to_all.23 = bf16[128,2,512]{2,1,0:T(2,128)(2,1)S(1)} all-to-all(bf16[128,2,512]{2,1,0:T(2,128)(2,1)S(1)} %reshape.23), channel_id=1, replica_groups=mesh['node'=128,'local'=8] {'node'}, dimensions={0} | all-to-all | bytes 524288 | tf_op jit(solution)/shard_map/all_to_all | solution.py:171
  136.0 0.1 reshape.24.rows_ref
  136.1 0.8 shard_map.68
  (1 shorter events, 0.0 us)
Async XLA Ops:
  0.0 7.6 %copy-start.1 = (bf16[32,512]{1,0:T(8,128)(2,1)S(1)}, bf16[32,512]{1,0:T(8,128)(2,1)}, u32[]{:S(2)}) copy-start(bf16[32,512]{1,0:T(8,128)(2,1)} %refs_3_.1) | copy-start | bytes 98308
  2.2 68.5 %collective-permute-start.2 = (bf16[512,2048]{1,0:T(8,128)(2,1)S(1)}, bf16[512,2048]{1,0:T(8,128)(2,1)}, u32[]{:S(2)}, u32[]{:S(2)}) collective-permute-start(bf16[512,2048]{1,0:T(8,128)(2,1)S(1)} %get-tuple-element.16.own_ref), channel_id=1, source_target_pairs={{0,1},{1,0},{2,3},{3,2},{4,5},{5,4},{6,7},{7,6},{9,10},{10,9},{11,... | collective-permute-start | bytes 6291464 | tf_op jit(solution)/shard_map/ppermute | solution.py:198
  7.6 6.1 %collective-permute-start = (bf16[32,512]{1,0:T(8,128)(2,1)S(1)}, bf16[32,512]{1,0:T(8,128)(2,1)S(1)}, u32[]{:S(2)}, u32[]{:S(2)}) collective-permute-start(bf16[32,512]{1,0:T(8,128)(2,1)S(1)} %copy-done.1), channel_id=1, source_target_pairs={{0,1},{1,0},{2,3},{3,2},{4,5},{5,4},{6,7},{7,6},{8,9},{9,8},{10,11... | collective-permute-start | bytes 98312 | tf_op jit(solution)/shard_map/ppermute | solution.py:176
  9.5 22.5 %collective-permute-start.1 = (bf16[32,512]{1,0:T(8,128)(2,1)S(1)}, bf16[32,512]{1,0:T(8,128)(2,1)S(1)}, u32[]{:S(2)}, u32[]{:S(2)}) collective-permute-start(bf16[32,512]{1,0:T(8,128)(2,1)S(1)} %copy-done.1), channel_id=1, source_target_pairs={{0,7},{1,2},{2,1},{3,4},{4,3},{5,6},{6,5},{7,0},{8,15},{9,10},{10,... | collective-permute-start | bytes 98312 | tf_op jit(solution)/shard_map/ppermute | solution.py:176
  72.8 39.6 %copy-start = (bf16[1,1024,512]{2,1,0:T(8,128)(2,1)S(1)}, bf16[1,1024,512]{2,1,0:T(8,128)(2,1)}, u32[]{:S(2)}) copy-start(bf16[1,1024,512]{2,1,0:T(8,128)(2,1)} %param.11) | copy-start | bytes 3145732

commit v6 on v5

--- a/solution.py
+++ b/solution.py
@@ -91,19 +91,13 @@
     out_ref[...] = (total_ref[...] + dot(theirs, pair_buf[...])).astype(jnp.bfloat16)
 
 
-def down_kernel(meta_ref, rows_ref, w_ref, out_ref, result_ref):
-    lines = rows_ref.shape[0]
-    ring = len(TEAM)
-    share = lines // ring
-    core = meta_ref[2]
-    result_ref[...] = dot(rows_ref[...], w_ref[...]).astype(jnp.bfloat16)
-    for member in range(len(TEAMS[0])):
-        total = 0.0
-        for place, team in enumerate(TEAMS):
-            seat = lax.rem(team[member] + core, ring)
-            block = result_ref[pl.ds(pl.multiple_of(seat * share, share), share), :]
-            total = total + dot(one_hot_rows(CAP * share, share, place, True), block)
-        out_ref[member * CAP * share : (member + 1) * CAP * share, :] = total.astype(jnp.bfloat16)
+def down_kernel(rows_ref, w_ref, out_ref):
+    half = rows_ref.shape[0] // CAP
+    total = 0.0
+    for place in range(CAP):
+        result = dot(rows_ref[place * half : (place + 1) * half, :], w_ref[...]).astype(jnp.bfloat16)
+        total = total + dot(one_hot_rows(CAP * half, half, place, True), result)
+    out_ref[...] = total.astype(jnp.bfloat16)
 
 
 def combine_kernel(high_ref, low_ref, rows_ref, out_ref):
@@ -160,6 +154,7 @@
         return ((place - core) % local_count ^ 1) + core
 
     team_groups = [[seat(node, label) for label in team] for node in nodes for team in TEAMS]
+    ring_groups = [[seat(node, label) for team in TEAMS for label in team] for node in nodes]
     pair_swap = [(seat(node, label), seat(node, label ^ 1)) for node in nodes for label in places]
     place = lax.axis_index("local")
     slot_of = [
@@ -177,8 +172,7 @@
         for core in range(CORES)
     ]
     lines = CAP * node_count
-    core = lax.axis_index("node") % CORES
-    meta = jnp.stack(slot_of + [core]).astype(jnp.int32)
+    meta = jnp.stack(slot_of).astype(jnp.int32)
     w_own, *tables = run(
         prepare_kernel,
         [(feat_width, 2 * hidden)] + [(lines, row_count)] * 5,
@@ -216,15 +210,8 @@
     active = (jax.nn.silu(total[:, :hidden]) * total[:, hidden:]).astype(jnp.bfloat16)
 
     copies = jnp.broadcast_to(active[None], (local_count, share, hidden))
-    rows = exchange(copies, "local").reshape(lines, hidden)
-    result = run(
-        down_kernel,
-        [(lines, feat_width)],
-        meta,
-        rows,
-        w_down[0],
-        scratch=[pltpu.VMEM((lines, feat_width), jnp.bfloat16)],
-    )
+    rows = exchange(copies, BOTH, ring_groups).reshape(lines, hidden)
+    result = run(down_kernel, [(lines, feat_width)], rows, w_down[0])
     returned = exchange(result.reshape(node_count, CAP, feat_width), "node").reshape(lines, feat_width)
     return run(combine_kernel, [(row_count, feat_width)], high, low, returned, final=True)
 

time: 137 us -> 135 us (0.985)
  blocking collectives: 99.8 us -> 97.4 us
    all_to_all x4, blocking collectives: 99.8 us -> 97.4 us  [exchange(): lax.all_to_all(array, axis, split_axis=0, concat_axis=0, tiled=True, axis...]
where the time goes in v6:
time: 135 us; the launch traced here: 134 us
  blocking collectives  97.4 us (72%)
  waiting for transfers between devices  18.3 us (14%)
  starting transfers between devices  11.4 us (8%)
  Pallas kernels  6.08 us (5%)
    all_to_all x4, blocking collectives, exchange(): lax.all_to_all(array, axis, split_axis=0, concat_axis=0, tiled=True, axis...  97.4 us
    ppermute x2, waiting for transfers between devices, body(): lax.ppermute(tokens, 'local', [(p, mate(p, core) % local_count) for p in...  18.3 us
    ppermute x2, starting transfers between devices, body(): lax.ppermute(tokens, 'local', [(p, mate(p, core) % local_count) for p in...  6.12 us
    pallas_call x5, Pallas kernels, run(): pl.pallas_call(kernel, in_specs=specs, out_specs=[pl.BlockSpec(memory_spa...  6.08 us
    ppermute x1, starting transfers between devices, body(): w_pair = lax.ppermute(w_own, BOTH, pair_swap)  5.32 us
  transfers between devices with their start and end apart: 3, of which 1 were waited for; matrix products, arithmetic and copies ran while one was open for 0% of the time, Pallas kernels for 0%

profile of v6, /device:TPU:1, one launch (start us, length us, event | category | flops | bytes accessed | tf_op | source)
XLA Modules:
  0.0 134.0 jit_solution(9139350727193848394)
XLA Ops:
  0.0 0.0 copy-start.1
  0.0 0.1 pad_add_fusion.meta_ref
  0.1 2.1 %shard_map.64 = (bf16[512,2048]{1,0:T(8,128)(2,1)S(1)}, bf16[256,32]{1,0:T(8,128)(2,1)S(1)}, bf16[256,32]{1,0:T(8,128)(2,1)S(1)}, bf16[256,32]{1,0:T(8,128)(2,1)...) custom-call(s32[2]{0:T(128)S(1)} %pad_add_fusion.meta_ref, s32[4,32]{1,0:T(4,128)} %bitcast.14, ...), custom_call_target="tpu_custom_call" | custom-call | tf_op jit(solution)/shard_map/pallas_call | solution.py:129
  2.2 5.3 %collective-permute-start.2 = (bf16[512,2048]{1,0:T(8,128)(2,1)S(1)}, bf16[512,2048]{1,0:T(8,128)(2,1)}, u32[]{:S(2)}, u32[]{:S(2)}) collective-permute-start(bf16[512,2048]{1,0:T(8,128)(2,1)S(1)} %get-tuple-element.16.own_ref), channel_id=1, source_target_pairs={{0,1},{1,0},{2,3},{3,2},{4,5},{5,4},{6,7},{7,6},{9,10},{10,9},{11,... | collective-permute-start | bytes 6291464 | tf_op jit(solution)/shard_map/ppermute | solution.py:192
  7.6 0.0 copy-done.1
  7.6 1.9 %collective-permute-start = (bf16[32,512]{1,0:T(8,128)(2,1)S(1)}, bf16[32,512]{1,0:T(8,128)(2,1)S(1)}, u32[]{:S(2)}, u32[]{:S(2)}) collective-permute-start(bf16[32,512]{1,0:T(8,128)(2,1)S(1)} %copy-done.1), channel_id=1, source_target_pairs={{0,1},{1,0},{2,3},{3,2},{4,5},{5,4},{6,7},{7,6},{8,9},{9,8},{10,11... | collective-permute-start | bytes 98312 | tf_op jit(solution)/shard_map/ppermute | solution.py:171
  9.5 4.2 %collective-permute-start.1 = (bf16[32,512]{1,0:T(8,128)(2,1)S(1)}, bf16[32,512]{1,0:T(8,128)(2,1)S(1)}, u32[]{:S(2)}, u32[]{:S(2)}) collective-permute-start(bf16[32,512]{1,0:T(8,128)(2,1)S(1)} %copy-done.1), channel_id=1, source_target_pairs={{0,7},{1,2},{2,1},{3,4},{4,3},{5,6},{6,5},{7,0},{8,15},{9,10},{10,... | collective-permute-start | bytes 98312 | tf_op jit(solution)/shard_map/ppermute | solution.py:171
  13.7 0.0 collective-permute-done.refs_4_
  13.7 18.3 %collective-permute-done.1.refs_5_ = bf16[32,512]{1,0:T(8,128)(2,1)S(1)} collective-permute-done((bf16[32,512]{1,0:T(8,128)(2,1)S(1)}, bf16[32,512]{1,0:T(8,128)(2,1)S(1)}, u32[]{:S(2)}, u32[]{:S(2)}) %collective-permute-start.1) | collective-permute-done | bytes 32800 | tf_op jit(solution)/shard_map/ppermute | solution.py:171
  32.0 0.3 shard_map.65
  32.3 0.1 reshape.19
  32.5 38.2 %all_to_all.20 = bf16[128,2,512]{2,1,0:T(2,128)(2,1)S(1)} all-to-all(bf16[128,2,512]{2,1,0:T(2,128)(2,1)S(1)} %reshape.19), channel_id=1, replica_groups=mesh['node'=128,'local'=8] {'node'}, dimensions={0} | all-to-all | bytes 524288 | tf_op jit(solution)/shard_map/all_to_all | solution.py:166
  70.7 0.1 reshape.20.rows_ref
  70.8 0.0 collective-permute-done.2.pair_ref
  70.8 2.1 %shard_map.66 = bf16[128,2048]{1,0:T(8,128)(2,1)S(1)} custom-call(bf16[256,512]{1,0:T(8,128)(2,1)S(1)} %reshape.20.rows_ref, bf16[512,2048]{1,0:T(8,128)(2,1)S(1)} %get-tuple-element.16.own_ref, bf16[512,2048]{1,0:T(8,128)(2,1)} %collective-permute-done.2.pair_ref), custom_call_target="tpu_custom_call" | custom-call | tf_op jit(solution)/shard_map/pallas_call | solution.py:129
  72.8 0.0 copy-start
  72.9 15.7 %all_to_all.21 = bf16[4,32,2048]{2,1,0:T(8,128)(2,1)S(1)} all-to-all(bf16[4,32,2048]{2,1,0:T(8,128)(2,1)S(1)} %bitcast.9), channel_id=1, replica_groups={{0,2,5,7},{1,3,4,6},{9,11,14,8},{10,12,13,15},{16,18,21,23},{17,19,20,2..., dimensions={0} | all-to-all | bytes 1048576 | tf_op jit(solution)/shard_map/all_to_all | solution.py:166
  88.5 0.1 convert_reduce_fusion
  88.7 0.1 broadcast_in_dim.2
  88.7 21.0 %all_to_all.22 = bf16[8,32,1024]{2,1,0:T(8,128)(2,1)S(1)} all-to-all(bf16[8,32,1024]{2,1,0:T(8,128)(2,1)S(1)} %broadcast_in_dim.2), channel_id=1, replica_groups={{0,2,5,7,1,3,4,6},{9,11,14,8,10,12,13,15},{16,18,21,23,17,19,20,22},{25..., dimensions={0} | all-to-all | bytes 1048576 | tf_op jit(solution)/shard_map/all_to_all | solution.py:166
  109.8 0.0 copy-done
  109.8 0.7 shard_map.67
  110.5 0.1 reshape.23
  110.6 22.5 %all_to_all.23 = bf16[128,2,512]{2,1,0:T(2,128)(2,1)S(1)} all-to-all(bf16[128,2,512]{2,1,0:T(2,128)(2,1)S(1)} %reshape.23), channel_id=1, replica_groups=mesh['node'=128,'local'=8] {'node'}, dimensions={0} | all-to-all | bytes 524288 | tf_op jit(solution)/shard_map/all_to_all | solution.py:166
  133.1 0.1 reshape.24.rows_ref
  133.2 0.8 shard_map.68
  (1 shorter events, 0.0 us)
Async XLA Ops:
  0.0 7.6 %copy-start.1 = (bf16[32,512]{1,0:T(8,128)(2,1)S(1)}, bf16[32,512]{1,0:T(8,128)(2,1)}, u32[]{:S(2)}) copy-start(bf16[32,512]{1,0:T(8,128)(2,1)} %refs_3_.1) | copy-start | bytes 98308
  2.2 68.5 %collective-permute-start.2 = (bf16[512,2048]{1,0:T(8,128)(2,1)S(1)}, bf16[512,2048]{1,0:T(8,128)(2,1)}, u32[]{:S(2)}, u32[]{:S(2)}) collective-permute-start(bf16[512,2048]{1,0:T(8,128)(2,1)S(1)} %get-tuple-element.16.own_ref), channel_id=1, source_target_pairs={{0,1},{1,0},{2,3},{3,2},{4,5},{5,4},{6,7},{7,6},{9,10},{10,9},{11,... | collective-permute-start | bytes 6291464 | tf_op jit(solution)/shard_map/ppermute | solution.py:192
  7.6 6.1 %collective-permute-start = (bf16[32,512]{1,0:T(8,128)(2,1)S(1)}, bf16[32,512]{1,0:T(8,128)(2,1)S(1)}, u32[]{:S(2)}, u32[]{:S(2)}) collective-permute-start(bf16[32,512]{1,0:T(8,128)(2,1)S(1)} %copy-done.1), channel_id=1, source_target_pairs={{0,1},{1,0},{2,3},{3,2},{4,5},{5,4},{6,7},{7,6},{8,9},{9,8},{10,11... | collective-permute-start | bytes 98312 | tf_op jit(solution)/shard_map/ppermute | solution.py:171
  9.5 22.5 %collective-permute-start.1 = (bf16[32,512]{1,0:T(8,128)(2,1)S(1)}, bf16[32,512]{1,0:T(8,128)(2,1)S(1)}, u32[]{:S(2)}, u32[]{:S(2)}) collective-permute-start(bf16[32,512]{1,0:T(8,128)(2,1)S(1)} %copy-done.1), channel_id=1, source_target_pairs={{0,7},{1,2},{2,1},{3,4},{4,3},{5,6},{6,5},{7,0},{8,15},{9,10},{10,... | collective-permute-start | bytes 98312 | tf_op jit(solution)/shard_map/ppermute | solution.py:171
  72.8 36.9 %copy-start = (bf16[1,1024,512]{2,1,0:T(8,128)(2,1)S(1)}, bf16[1,1024,512]{2,1,0:T(8,128)(2,1)}, u32[]{:S(2)}) copy-start(bf16[1,1024,512]{2,1,0:T(8,128)(2,1)} %param.11) | copy-start | bytes 3145732

commit v7 on v6

--- a/solution.py
+++ b/solution.py
@@ -24,24 +24,15 @@
     return same.astype(jnp.float32).astype(jnp.bfloat16)
 
 
-def prepare_kernel(
-    meta_ref, ids_hbm, mix_hbm, gate_ref, up_ref,
-    joined_ref, own_ref, first_ref, second_ref, high_ref, low_ref,
-    ids_ref, mix_ref, sems,
+def tables_kernel(
+    meta_ref, ids_hbm, mix_hbm, own_ref, first_ref, second_ref, high_ref, low_ref, ids_ref, mix_ref, sems
 ):
-    hidden = gate_ref.shape[1]
     tables = [
-        pltpu.make_async_copy(source, target, sems.at[2 + index])
+        pltpu.make_async_copy(source, target, sems.at[index])
         for index, (source, target) in enumerate(((ids_hbm, ids_ref), (mix_hbm, mix_ref)))
     ]
     for table in tables:
         table.start()
-    joins = [
-        pltpu.make_async_copy(ref, joined_ref.at[:, pl.ds(index * hidden, hidden)], sems.at[index])
-        for index, ref in enumerate((gate_ref, up_ref))
-    ]
-    for join in joins:
-        join.start()
     for table in tables:
         table.wait()
     lines, row_count = high_ref.shape
@@ -68,8 +59,6 @@
     theirs = jnp.where(part == 1, chosen, 0.0)
     for core, ref in enumerate((first_ref, second_ref)):
         ref[...] = jnp.where(parity == core, theirs, 0.0).astype(jnp.bfloat16)
-    for join in joins:
-        join.wait()
 
 
 def gather_kernel(*refs):
@@ -79,16 +68,25 @@
     out_ref[...] = total.astype(jnp.bfloat16)
 
 
-def project_kernel(rows_ref, own_ref, pair_ref, out_ref, total_ref, pair_buf, sem):
-    copy = pltpu.make_async_copy(pair_ref, pair_buf, sem)
-    copy.start()
+def project_kernel(rows_ref, *refs):
+    own, pair, (out_ref, total_ref), bufs, sems = refs[:2], refs[2:4], refs[4:6], refs[6:8], refs[8]
+    copies = [
+        pltpu.make_async_copy(source, target, sems.at[index])
+        for index, (source, target) in enumerate(zip(pair, bufs))
+    ]
+    for copy in copies:
+        copy.start()
     lines = rows_ref.shape[0]
+    hidden = bufs[0].shape[1]
     rows = rows_ref[...]
     mine = dot(one_hot_rows(lines // CAP, lines, 0), rows).astype(jnp.bfloat16)
     theirs = dot(one_hot_rows(lines // CAP, lines, 1), rows).astype(jnp.bfloat16)
-    total_ref[...] = dot(mine, own_ref[...])
-    copy.wait()
-    out_ref[...] = (total_ref[...] + dot(theirs, pair_buf[...])).astype(jnp.bfloat16)
+    for index, ref in enumerate(own):
+        total_ref[:, index * hidden : (index + 1) * hidden] = dot(mine, ref[...])
+    for index, (copy, buf) in enumerate(zip(copies, bufs)):
+        columns = slice(index * hidden, (index + 1) * hidden)
+        copy.wait()
+        out_ref[:, columns] = (total_ref[:, columns] + dot(theirs, buf[...])).astype(jnp.bfloat16)
 
 
 def down_kernel(rows_ref, w_ref, out_ref):
@@ -167,42 +165,43 @@
             array, axis, split_axis=0, concat_axis=0, tiled=True, axis_index_groups=groups
         )
 
+    gate_pair = lax.ppermute(w_gate[0], BOTH, pair_swap)
+    up_pair = lax.ppermute(w_up[0], BOTH, pair_swap)
     tokens_pair = [
         lax.ppermute(tokens, "local", [(p, mate(p, core) % local_count) for p in places])
         for core in range(CORES)
     ]
     lines = CAP * node_count
     meta = jnp.stack(slot_of).astype(jnp.int32)
-    w_own, *tables = run(
-        prepare_kernel,
-        [(feat_width, 2 * hidden)] + [(lines, row_count)] * 5,
+    *picks, high, low = run(
+        tables_kernel,
+        [(lines, row_count)] * 5,
         meta,
         node_ids.T,
         mix_weights.T,
-        w_gate[0],
-        w_up[0],
-        hbm=(1, 2, 3, 4),
+        hbm=(1, 2),
         scratch=[
             pltpu.VMEM(node_ids.shape[::-1], jnp.int32),
             pltpu.VMEM(mix_weights.shape[::-1], jnp.float32),
-            pltpu.SemaphoreType.DMA((4,)),
+            pltpu.SemaphoreType.DMA((2,)),
         ],
     )
-    picks, (high, low) = tables[:3], tables[3:]
-    w_pair = lax.ppermute(w_own, BOTH, pair_swap)
     outbound = run(gather_kernel, [(lines, feat_width)], *picks, tokens, *tokens_pair)
     inbound = exchange(outbound.reshape(node_count, CAP, feat_width), "node")
     sums = run(
         project_kernel,
         [(node_count, 2 * hidden)],
         inbound.reshape(lines, feat_width),
-        w_own,
-        w_pair,
-        hbm=(2,),
+        w_gate[0],
+        w_up[0],
+        gate_pair,
+        up_pair,
+        hbm=(3, 4),
         scratch=[
             pltpu.VMEM((node_count, 2 * hidden), jnp.float32),
-            pltpu.VMEM((feat_width, 2 * hidden), jnp.bfloat16),
-            pltpu.SemaphoreType.DMA,
+            pltpu.VMEM((feat_width, hidden), jnp.bfloat16),
+            pltpu.VMEM((feat_width, hidden), jnp.bfloat16),
+            pltpu.SemaphoreType.DMA((2,)),
         ],
     )
     parts = exchange(sums.reshape(members, share, 2 * hidden), BOTH, team_groups)

time: 135 us -> 133 us (0.985)
  waiting for transfers between devices: 18.3 us -> 15 us
  starting transfers between devices: 11.4 us -> 13.7 us
    ppermute x2, waiting for transfers between devices: 18.3 us -> 15 us  [body(): lax.ppermute(tokens, 'local', [(p, mate(p, core) % local_count) for p in...]
    ppermute x1 -> x2, starting transfers between devices: 5.32 us -> 7.23 us  [the longest x1 5.31 us: body(): gate_pair = lax.ppermute(w_gate[0], BOTH, pair_swap)]
  transfers between devices with their start and end apart: 3 -> 4, of which waited for: 1 -> 1; matrix products, arithmetic and copies ran while one was open for 0% -> 0% of each run, Pallas kernels for 0% -> 1%
where the time goes in v7:
time: 133 us; the launch traced here: 132 us
  blocking collectives  97.2 us (73%)
  waiting for transfers between devices  15 us (11%)
  starting transfers between devices  13.7 us (10%)
  Pallas kernels  5.28 us (4%)
    all_to_all x4, blocking collectives, exchange(): lax.all_to_all(array, axis, split_axis=0, concat_axis=0, tiled=True, axis...  97.2 us
    ppermute x2, waiting for transfers between devices, body(): lax.ppermute(tokens, 'local', [(p, mate(p, core) % local_count) for p in...  15 us
    ppermute x2, starting transfers between devices, body(): lax.ppermute(tokens, 'local', [(p, mate(p, core) % local_count) for p in...  6.49 us
    ppermute x1, starting transfers between devices, body(): gate_pair = lax.ppermute(w_gate[0], BOTH, pair_swap)  5.31 us
    pallas_call x5, Pallas kernels, run(): pl.pallas_call(kernel, in_specs=specs, out_specs=[pl.BlockSpec(memory_spa...  5.28 us
  transfers between devices with their start and end apart: 4, of which 1 were waited for; matrix products, arithmetic and copies ran while one was open for 0% of the time, Pallas kernels for 1%

profile of v7, /device:TPU:1, one launch (start us, length us, event | category | flops | bytes accessed | tf_op | source)
XLA Modules:
  0.0 132.0 jit_solution(18441998583879375719)
XLA Ops:
  0.0 5.3 %collective-permute-start.2 = (bf16[512,1024]{1,0:T(8,128)(2,1)}, bf16[512,1024]{1,0:T(8,128)(2,1)}, u32[]{:S(2)}, u32[]{:S(2)}) collective-permute-start(bf16[512,1024]{1,0:T(8,128)(2,1)} %bitcast.11), channel_id=1, source_target_pairs={{0,1},{1,0},{2,3},{3,2},{4,5},{5,4},{6,7},{7,6},{9,10},{10,9},{11,... | collective-permute-start | bytes 3145736 | tf_op jit(solution)/shard_map/ppermute | solution.py:168
  5.3 0.0 copy-start.3
  5.3 1.9 %collective-permute-start.3 = (bf16[512,1024]{1,0:T(8,128)(2,1)}, bf16[512,1024]{1,0:T(8,128)(2,1)}, u32[]{:S(2)}, u32[]{:S(2)}) collective-permute-start(bf16[512,1024]{1,0:T(8,128)(2,1)} %bitcast.13), channel_id=1, source_target_pairs={{0,1},{1,0},{2,3},{3,2},{4,5},{5,4},{6,7},{7,6},{9,10},{10,9},{11,... | collective-permute-start | bytes 3145736 | tf_op jit(solution)/shard_map/ppermute | solution.py:169
  7.3 2.0 %collective-permute-start = (bf16[32,512]{1,0:T(8,128)(2,1)}, bf16[32,512]{1,0:T(8,128)(2,1)S(1)}, u32[]{:S(2)}, u32[]{:S(2)}) collective-permute-start(bf16[32,512]{1,0:T(8,128)(2,1)} %refs_3_.1), channel_id=1, source_target_pairs={{0,1},{1,0},{2,3},{3,2},{4,5},{5,4},{6,7},{7,6},{8,9},{9,8},{10,11... | collective-permute-start | bytes 98312 | tf_op jit(solution)/shard_map/ppermute | solution.py:171
  9.2 4.5 %collective-permute-start.1 = (bf16[32,512]{1,0:T(8,128)(2,1)}, bf16[32,512]{1,0:T(8,128)(2,1)S(1)}, u32[]{:S(2)}, u32[]{:S(2)}) collective-permute-start(bf16[32,512]{1,0:T(8,128)(2,1)} %refs_3_.1), channel_id=1, source_target_pairs={{0,7},{1,2},{2,1},{3,4},{4,3},{5,6},{6,5},{7,0},{8,15},{9,10},{10,... | collective-permute-start | bytes 98312 | tf_op jit(solution)/shard_map/ppermute | solution.py:171
  13.8 0.1 pad_add_fusion.meta_ref
  13.9 1.5 %shard_map.64 = (bf16[256,32]{1,0:T(8,128)(2,1)S(1)}, bf16[256,32]{1,0:T(8,128)(2,1)S(1)}, bf16[256,32]{1,0:T(8,128)(2,1)S(1)}, bf16[256,32]{1,0:T(8,128)(2,1)S(1)}, bf16[256,32]{1,0:T(8,128)(2,1)S(1)}) custom-call(s32[2]{0:T(128)S(1)} %pad_add_fusion.meta_ref, s32[4,32]{1,0:T(4,128)} %bitcast.16, f32[4,32]{1,0:T(4,128)} %bitcast.17), custom_call_target="tpu_custom_call" | custom-call | tf_op jit(solution)/shard_map/pallas_call | solution.py:127
  15.4 0.0 collective-permute-done.refs_4_
  15.4 15.0 %collective-permute-done.1.refs_5_ = bf16[32,512]{1,0:T(8,128)(2,1)S(1)} collective-permute-done((bf16[32,512]{1,0:T(8,128)(2,1)}, bf16[32,512]{1,0:T(8,128)(2,1)S(1)}, u32[]{:S(2)}, u32[]{:S(2)}) %collective-permute-start.1) | collective-permute-done | bytes 32800 | tf_op jit(solution)/shard_map/ppermute | solution.py:171
  30.4 0.0 copy-done.3
  30.4 0.0 copy-start
  30.4 0.0 copy-start.1
  30.4 0.3 shard_map.65
  30.7 0.1 reshape.19
  30.8 37.9 %all_to_all.20 = bf16[128,2,512]{2,1,0:T(2,128)(2,1)S(1)} all-to-all(bf16[128,2,512]{2,1,0:T(2,128)(2,1)S(1)} %reshape.19), channel_id=1, replica_groups=mesh['node'=128,'local'=8] {'node'}, dimensions={0} | all-to-all | bytes 524288 | tf_op jit(solution)/shard_map/all_to_all | solution.py:164
  68.8 0.1 reshape.20.rows_ref
  68.9 0.0 collective-permute-done.2.refs_2_
  68.9 0.0 collective-permute-done.3.refs_3_
  68.9 0.0 copy-done
  68.9 0.0 copy-done.1
  68.9 1.9 %shard_map.66 = bf16[128,2048]{1,0:T(8,128)(2,1)S(1)} custom-call(bf16[256,512]{1,0:T(8,128)(2,1)S(1)} %reshape.20.rows_ref, bf16[512,1024]{1,0:T(8,128)(2,1)S(1)} %bitcast.12, bf16[512,1024]{1,0:T(8,128)(2,1)S(1)} %bitcast.14, bf16[512,1024]{1,0:T(8,128)(2,1)} %collective-permute-done.2.refs_2_, bf16[512,1024]{1,0:T(8,128)(2,1)} %collective-permute-done.3.refs_3_), custom_call_target="tpu_custom_call" | custom-call | tf_op jit(solution)/shard_map/pallas_call | solution.py:127
  70.8 15.5 %all_to_all.21 = bf16[4,32,2048]{2,1,0:T(8,128)(2,1)S(1)} all-to-all(bf16[4,32,2048]{2,1,0:T(8,128)(2,1)S(1)} %bitcast.9), channel_id=1, replica_groups={{0,2,5,7},{1,3,4,6},{9,11,14,8},{10,12,13,15},{16,18,21,23},{17,19,20,2..., dimensions={0} | all-to-all | bytes 1048576 | tf_op jit(solution)/shard_map/all_to_all | solution.py:164
  86.4 0.1 convert_reduce_fusion
  86.4 0.0 copy-start.2
  86.5 0.1 broadcast_in_dim.2
  86.6 21.2 %all_to_all.22 = bf16[8,32,1024]{2,1,0:T(8,128)(2,1)S(1)} all-to-all(bf16[8,32,1024]{2,1,0:T(8,128)(2,1)S(1)} %broadcast_in_dim.2), channel_id=1, replica_groups={{0,2,5,7,1,3,4,6},{9,11,14,8,10,12,13,15},{16,18,21,23,17,19,20,22},{25..., dimensions={0} | all-to-all | bytes 1048576 | tf_op jit(solution)/shard_map/all_to_all | solution.py:164
  107.7 0.0 copy-done.2
  107.7 0.7 shard_map.67
  108.4 0.1 reshape.23
  108.6 22.5 %all_to_all.23 = bf16[128,2,512]{2,1,0:T(2,128)(2,1)S(1)} all-to-all(bf16[128,2,512]{2,1,0:T(2,128)(2,1)S(1)} %reshape.23), channel_id=1, replica_groups=mesh['node'=128,'local'=8] {'node'}, dimensions={0} | all-to-all | bytes 524288 | tf_op jit(solution)/shard_map/all_to_all | solution.py:164
  131.1 0.1 reshape.24.rows_ref
  131.2 0.8 shard_map.68
  (1 shorter events, 0.0 us)
Async XLA Ops:
  0.0 68.9 %collective-permute-start.2 = (bf16[512,1024]{1,0:T(8,128)(2,1)}, bf16[512,1024]{1,0:T(8,128)(2,1)}, u32[]{:S(2)}, u32[]{:S(2)}) collective-permute-start(bf16[512,1024]{1,0:T(8,128)(2,1)} %bitcast.11), channel_id=1, source_target_pairs={{0,1},{1,0},{2,3},{3,2},{4,5},{5,4},{6,7},{7,6},{9,10},{10,9},{11,... | collective-permute-start | bytes 3145736 | tf_op jit(solution)/shard_map/ppermute | solution.py:168
  5.3 25.1 %copy-start.3 = (bf16[32,512]{1,0:T(8,128)(2,1)S(1)}, bf16[32,512]{1,0:T(8,128)(2,1)}, u32[]{:S(2)}) copy-start(bf16[32,512]{1,0:T(8,128)(2,1)} %refs_3_.1) | copy-start | bytes 98308
  5.3 63.6 %collective-permute-start.3 = (bf16[512,1024]{1,0:T(8,128)(2,1)}, bf16[512,1024]{1,0:T(8,128)(2,1)}, u32[]{:S(2)}, u32[]{:S(2)}) collective-permute-start(bf16[512,1024]{1,0:T(8,128)(2,1)} %bitcast.13), channel_id=1, source_target_pairs={{0,1},{1,0},{2,3},{3,2},{4,5},{5,4},{6,7},{7,6},{9,10},{10,9},{11,... | collective-permute-start | bytes 3145736 | tf_op jit(solution)/shard_map/ppermute | solution.py:169
  7.3 8.1 %collective-permute-start = (bf16[32,512]{1,0:T(8,128)(2,1)}, bf16[32,512]{1,0:T(8,128)(2,1)S(1)}, u32[]{:S(2)}, u32[]{:S(2)}) collective-permute-start(bf16[32,512]{1,0:T(8,128)(2,1)} %refs_3_.1), channel_id=1, source_target_pairs={{0,1},{1,0},{2,3},{3,2},{4,5},{5,4},{6,7},{7,6},{8,9},{9,8},{10,11... | collective-permute-start | bytes 98312 | tf_op jit(solution)/shard_map/ppermute | solution.py:171
  9.2 21.1 %collective-permute-start.1 = (bf16[32,512]{1,0:T(8,128)(2,1)}, bf16[32,512]{1,0:T(8,128)(2,1)S(1)}, u32[]{:S(2)}, u32[]{:S(2)}) collective-permute-start(bf16[32,512]{1,0:T(8,128)(2,1)} %refs_3_.1), channel_id=1, source_target_pairs={{0,7},{1,2},{2,1},{3,4},{4,3},{5,6},{6,5},{7,0},{8,15},{9,10},{10,... | collective-permute-start | bytes 98312 | tf_op jit(solution)/shard_map/ppermute | solution.py:171
  30.4 38.5 %copy-start = (bf16[1,512,1024]{2,1,0:T(8,128)(2,1)S(1)}, bf16[1,512,1024]{2,1,0:T(8,128)(2,1)}, u32[]{:S(2)}) copy-start(bf16[1,512,1024]{2,1,0:T(8,128)(2,1)} %param.9) | copy-start | bytes 3145732
  30.4 38.5 %copy-start.1 = (bf16[1,512,1024]{2,1,0:T(8,128)(2,1)S(1)}, bf16[1,512,1024]{2,1,0:T(8,128)(2,1)}, u32[]{:S(2)}) copy-start(bf16[1,512,1024]{2,1,0:T(8,128)(2,1)} %param.10) | copy-start | bytes 3145732
  86.4 21.3 %copy-start.2 = (bf16[1,1024,512]{2,1,0:T(8,128)(2,1)S(1)}, bf16[1,1024,512]{2,1,0:T(8,128)(2,1)}, u32[]{:S(2)}) copy-start(bf16[1,1024,512]{2,1,0:T(8,128)(2,1)} %param.11) | copy-start | bytes 3145732

commit v8 on v7

--- a/solution.py
+++ b/solution.py
@@ -24,8 +24,8 @@
     return same.astype(jnp.float32).astype(jnp.bfloat16)
 
 
-def tables_kernel(
-    meta_ref, ids_hbm, mix_hbm, own_ref, first_ref, second_ref, high_ref, low_ref, ids_ref, mix_ref, sems
+def route_kernel(
+    slot_ref, ids_hbm, mix_hbm, own_ref, first_ref, second_ref, out_ref, high_ref, low_ref, ids_ref, mix_ref, sems
 ):
     tables = [
         pltpu.make_async_copy(source, target, sems.at[index])
@@ -33,14 +33,14 @@
     ]
     for table in tables:
         table.start()
-    for table in tables:
-        table.wait()
     lines, row_count = high_ref.shape
     line = lax.broadcasted_iota(jnp.int32, (lines, row_count), 0)
     expert, part = line // CAP, line % CAP
     parity = expert % CORES
     hit = jnp.zeros((lines, row_count), jnp.float32)
     weight = jnp.zeros((lines, row_count), jnp.float32)
+    for table in tables:
+        table.wait()
     for pick in range(ids_ref.shape[0]):
         match = ids_ref[pick : pick + 1, :] == expert
         hit = jnp.where(match, 1.0, hit)
@@ -53,40 +53,33 @@
     high = combine.astype(jnp.bfloat16)
     high_ref[...] = high
     low_ref[...] = (combine - high.astype(jnp.float32)).astype(jnp.bfloat16)
-    slot = jnp.where(parity == 0, meta_ref[0], meta_ref[1]).astype(jnp.float32)
+    slot = jnp.where(parity == 0, slot_ref[0], slot_ref[1]).astype(jnp.float32)
     chosen = jnp.where(rank == slot, hit, 0.0)
-    own_ref[...] = jnp.where(part == 0, chosen, 0.0).astype(jnp.bfloat16)
+    total = dot(jnp.where(part == 0, chosen, 0.0).astype(jnp.bfloat16), own_ref[...])
     theirs = jnp.where(part == 1, chosen, 0.0)
     for core, ref in enumerate((first_ref, second_ref)):
-        ref[...] = jnp.where(parity == core, theirs, 0.0).astype(jnp.bfloat16)
-
-
-def gather_kernel(*refs):
-    out_ref = refs[-1]
-    picks, slices = refs[: len(refs) // 2], refs[len(refs) // 2 : -1]
-    total = sum(dot(pick[...], rows[...]) for pick, rows in zip(picks, slices))
+        total = total + dot(jnp.where(parity == core, theirs, 0.0).astype(jnp.bfloat16), ref[...])
     out_ref[...] = total.astype(jnp.bfloat16)
 
 
 def project_kernel(rows_ref, *refs):
-    own, pair, (out_ref, total_ref), bufs, sems = refs[:2], refs[2:4], refs[4:6], refs[6:8], refs[8]
+    gates, ups, out_ref, bufs, sems = refs[0:4:2], refs[1:4:2], refs[4], refs[5:7], refs[7]
     copies = [
         pltpu.make_async_copy(source, target, sems.at[index])
-        for index, (source, target) in enumerate(zip(pair, bufs))
+        for index, (source, target) in enumerate(zip(ups, bufs))
     ]
     for copy in copies:
         copy.start()
     lines = rows_ref.shape[0]
     hidden = bufs[0].shape[1]
     rows = rows_ref[...]
-    mine = dot(one_hot_rows(lines // CAP, lines, 0), rows).astype(jnp.bfloat16)
-    theirs = dot(one_hot_rows(lines // CAP, lines, 1), rows).astype(jnp.bfloat16)
-    for index, ref in enumerate(own):
-        total_ref[:, index * hidden : (index + 1) * hidden] = dot(mine, ref[...])
-    for index, (copy, buf) in enumerate(zip(copies, bufs)):
-        columns = slice(index * hidden, (index + 1) * hidden)
+    parts = [dot(one_hot_rows(lines // CAP, lines, place), rows).astype(jnp.bfloat16) for place in range(CAP)]
+    out_ref[:, :hidden] = sum(dot(part, ref[...]) for part, ref in zip(parts, gates)).astype(jnp.bfloat16)
+    total = 0.0
+    for part, copy, buf in zip(parts, copies, bufs):
         copy.wait()
-        out_ref[:, columns] = (total_ref[:, columns] + dot(theirs, buf[...])).astype(jnp.bfloat16)
+        total = total + dot(part, buf[...])
+    out_ref[:, hidden:] = total.astype(jnp.bfloat16)
 
 
 def down_kernel(rows_ref, w_ref, out_ref):
@@ -173,12 +166,14 @@
     ]
     lines = CAP * node_count
     meta = jnp.stack(slot_of).astype(jnp.int32)
-    *picks, high, low = run(
-        tables_kernel,
-        [(lines, row_count)] * 5,
+    outbound, high, low = run(
+        route_kernel,
+        [(lines, feat_width), (lines, row_count), (lines, row_count)],
         meta,
         node_ids.T,
         mix_weights.T,
+        tokens,
+        *tokens_pair,
         hbm=(1, 2),
         scratch=[
             pltpu.VMEM(node_ids.shape[::-1], jnp.int32),
@@ -186,7 +181,6 @@
             pltpu.SemaphoreType.DMA((2,)),
         ],
     )
-    outbound = run(gather_kernel, [(lines, feat_width)], *picks, tokens, *tokens_pair)
     inbound = exchange(outbound.reshape(node_count, CAP, feat_width), "node")
     sums = run(
         project_kernel,
@@ -196,9 +190,8 @@
         w_up[0],
         gate_pair,
         up_pair,
-        hbm=(3, 4),
+        hbm=(2, 4),
         scratch=[
-            pltpu.VMEM((node_count, 2 * hidden), jnp.float32),
             pltpu.VMEM((feat_width, hidden), jnp.bfloat16),
             pltpu.VMEM((feat_width, hidden), jnp.bfloat16),
             pltpu.SemaphoreType.DMA((2,)),

time: 133 us -> 135 us (1.015)
  waiting for transfers between devices: 15 us -> 16.5 us
    ppermute x2, waiting for transfers between devices: 15 us -> 16.5 us  [body(): lax.ppermute(tokens, 'local', [(p, mate(p, core) % local_count) for p in...]
    pallas_call x5 -> x4, Pallas kernels: 5.28 us -> 5.66 us  [run(): pl.pallas_call(kernel, in_specs=specs, out_specs=[pl.BlockSpec(memory_spa...]
where the time goes in v8:
time: 135 us
  blocking collectives  97 us (72%)
  waiting for transfers between devices  16.5 us (12%)
  starting transfers between devices  13.9 us (10%)
  Pallas kernels  5.66 us (4%)
    all_to_all x4, blocking collectives, exchange(): lax.all_to_all(array, axis, split_axis=0, concat_axis=0, tiled=True, axis...  97 us
    ppermute x2, waiting for transfers between devices, body(): lax.ppermute(tokens, 'local', [(p, mate(p, core) % local_count) for p in...  16.5 us
    ppermute x2, starting transfers between devices, body(): lax.ppermute(tokens, 'local', [(p, mate(p, core) % local_count) for p in...  6.5 us
    pallas_call x4, Pallas kernels, run(): pl.pallas_call(kernel, in_specs=specs, out_specs=[pl.BlockSpec(memory_spa...  5.66 us
    ppermute x1, starting transfers between devices, body(): gate_pair = lax.ppermute(w_gate[0], BOTH, pair_swap)  5.44 us
  transfers between devices with their start and end apart: 4, of which 1 were waited for; matrix products, arithmetic and copies ran while one was open for 0% of the time, Pallas kernels for 1%

profile of v8, /device:TPU:1, one launch (start us, length us, event | category | flops | bytes accessed | tf_op | source)
XLA Modules:
  0.0 134.6 jit_solution(9103948125822567359)
XLA Ops:
  0.0 0.0 copy-start
  0.0 5.4 %collective-permute-start.2 = (bf16[512,1024]{1,0:T(8,128)(2,1)}, bf16[512,1024]{1,0:T(8,128)(2,1)S(1)}, u32[]{:S(2)}, u32[]{:S(2)}) collective-permute-start(bf16[512,1024]{1,0:T(8,128)(2,1)} %bitcast.11), channel_id=1, source_target_pairs={{0,1},{1,0},{2,3},{3,2},{4,5},{5,4},{6,7},{7,6},{9,10},{10,9},{11,... | collective-permute-start | bytes 3145736 | tf_op jit(solution)/shard_map/ppermute | solution.py:161
  5.4 1.9 %collective-permute-start.3 = (bf16[512,1024]{1,0:T(8,128)(2,1)}, bf16[512,1024]{1,0:T(8,128)(2,1)}, u32[]{:S(2)}, u32[]{:S(2)}) collective-permute-start(bf16[512,1024]{1,0:T(8,128)(2,1)} %bitcast.14), channel_id=1, source_target_pairs={{0,1},{1,0},{2,3},{3,2},{4,5},{5,4},{6,7},{7,6},{9,10},{10,9},{11,... | collective-permute-start | bytes 3145736 | tf_op jit(solution)/shard_map/ppermute | solution.py:162
  7.4 2.0 %collective-permute-start = (bf16[32,512]{1,0:T(8,128)(2,1)}, bf16[32,512]{1,0:T(8,128)(2,1)S(1)}, u32[]{:S(2)}, u32[]{:S(2)}) collective-permute-start(bf16[32,512]{1,0:T(8,128)(2,1)} %own_ref.1), channel_id=1, source_target_pairs={{0,1},{1,0},{2,3},{3,2},{4,5},{5,4},{6,7},{7,6},{8,9},{9,8},{10,11... | collective-permute-start | bytes 98312 | tf_op jit(solution)/shard_map/ppermute | solution.py:164
  9.4 4.5 %collective-permute-start.1 = (bf16[32,512]{1,0:T(8,128)(2,1)}, bf16[32,512]{1,0:T(8,128)(2,1)S(1)}, u32[]{:S(2)}, u32[]{:S(2)}) collective-permute-start(bf16[32,512]{1,0:T(8,128)(2,1)} %own_ref.1), channel_id=1, source_target_pairs={{0,7},{1,2},{2,1},{3,4},{4,3},{5,6},{6,5},{7,0},{8,15},{9,10},{10,... | collective-permute-start | bytes 98312 | tf_op jit(solution)/shard_map/ppermute | solution.py:164
  13.9 0.1 pad_add_fusion.slot_ref
  14.0 0.0 collective-permute-done.first_ref
  14.0 16.5 %collective-permute-done.1.second_ref = bf16[32,512]{1,0:T(8,128)(2,1)S(1)} collective-permute-done((bf16[32,512]{1,0:T(8,128)(2,1)}, bf16[32,512]{1,0:T(8,128)(2,1)S(1)}, u32[]{:S(2)}, u32[]{:S(2)}) %collective-permute-start.1) | collective-permute-done | bytes 32800 | tf_op jit(solution)/shard_map/ppermute | solution.py:164
  30.5 0.0 copy-start.2
  30.5 0.8 copy-done.2
  31.3 1.8 %shard_map.64 = (bf16[256,512]{1,0:T(8,128)(2,1)S(1)}, bf16[256,32]{1,0:T(8,128)(2,1)S(1)}, bf16[256,32]{1,0:T(8,128)(2,1)S(1)}) custom-call(s32[2]{0:T(128)S(1)} %pad_add_fusion.slot_ref, s32[4,32]{1,0:T(4,128)} %bitcast.16, f32[4,32]{1,0:T(4,128)} %bitcast.17, bf16[32,512]{1,0:T(8,128)(2,1)S(1)} %copy-done.2, ...), custom_call_target="tpu_custom_call" | custom-call | tf_op jit(solution)/shard_map/pallas_call | solution.py:120
  33.0 0.1 reshape.19
  33.1 37.8 %all_to_all.20 = bf16[128,2,512]{2,1,0:T(2,128)(2,1)S(1)} all-to-all(bf16[128,2,512]{2,1,0:T(2,128)(2,1)S(1)} %reshape.19), channel_id=1, replica_groups=mesh['node'=128,'local'=8] {'node'}, dimensions={0} | all-to-all | bytes 524288 | tf_op jit(solution)/shard_map/all_to_all | solution.py:157
  70.9 0.1 reshape.20.rows_ref
  71.0 0.0 collective-permute-done.2.refs_2_
  71.1 0.0 collective-permute-done.3.refs_3_
  71.1 0.0 copy-done
  71.1 2.4 %shard_map.65 = bf16[128,2048]{1,0:T(8,128)(2,1)S(1)} custom-call(bf16[256,512]{1,0:T(8,128)(2,1)S(1)} %reshape.20.rows_ref, bf16[512,1024]{1,0:T(8,128)(2,1)S(1)} %bitcast.12, bf16[512,1024]{1,0:T(8,128)(2,1)} %bitcast.15, bf16[512,1024]{1,0:T(8,128)(2,1)S(1)} %collective-permute-done.2.refs_2_, bf16[512,1024]{1,0:T(8,128)(2,1)} %collective-permute-done.3.refs_3_), custom_call_target="tpu_custom_call" | custom-call | tf_op jit(solution)/shard_map/pallas_call | solution.py:120
  73.4 15.5 %all_to_all.21 = bf16[4,32,2048]{2,1,0:T(8,128)(2,1)S(1)} all-to-all(bf16[4,32,2048]{2,1,0:T(8,128)(2,1)S(1)} %bitcast.9), channel_id=1, replica_groups={{0,2,5,7},{1,3,4,6},{9,11,14,8},{10,12,13,15},{16,18,21,23},{17,19,20,2..., dimensions={0} | all-to-all | bytes 1048576 | tf_op jit(solution)/shard_map/all_to_all | solution.py:157
  89.0 0.1 convert_reduce_fusion
  89.1 0.0 copy-start.1
  89.1 0.1 broadcast_in_dim.2
  89.2 21.2 %all_to_all.22 = bf16[8,32,1024]{2,1,0:T(8,128)(2,1)S(1)} all-to-all(bf16[8,32,1024]{2,1,0:T(8,128)(2,1)S(1)} %broadcast_in_dim.2), channel_id=1, replica_groups={{0,2,5,7,1,3,4,6},{9,11,14,8,10,12,13,15},{16,18,21,23,17,19,20,22},{25..., dimensions={0} | all-to-all | bytes 1048576 | tf_op jit(solution)/shard_map/all_to_all | solution.py:157
  110.4 0.0 copy-done.1
  110.4 0.7 shard_map.66
  111.1 0.1 reshape.23
  111.2 22.5 %all_to_all.23 = bf16[128,2,512]{2,1,0:T(2,128)(2,1)S(1)} all-to-all(bf16[128,2,512]{2,1,0:T(2,128)(2,1)S(1)} %reshape.23), channel_id=1, replica_groups=mesh['node'=128,'local'=8] {'node'}, dimensions={0} | all-to-all | bytes 524288 | tf_op jit(solution)/shard_map/all_to_all | solution.py:157
  133.7 0.1 reshape.24.rows_ref
  133.8 0.8 shard_map.67
  (1 shorter events, 0.0 us)
Async XLA Ops:
  0.0 71.1 %copy-start = (bf16[1,512,1024]{2,1,0:T(8,128)(2,1)S(1)}, bf16[1,512,1024]{2,1,0:T(8,128)(2,1)}, u32[]{:S(2)}) copy-start(bf16[1,512,1024]{2,1,0:T(8,128)(2,1)} %param.9) | copy-start | bytes 3145732
  0.0 71.0 %collective-permute-start.2 = (bf16[512,1024]{1,0:T(8,128)(2,1)}, bf16[512,1024]{1,0:T(8,128)(2,1)S(1)}, u32[]{:S(2)}, u32[]{:S(2)}) collective-permute-start(bf16[512,1024]{1,0:T(8,128)(2,1)} %bitcast.11), channel_id=1, source_target_pairs={{0,1},{1,0},{2,3},{3,2},{4,5},{5,4},{6,7},{7,6},{9,10},{10,9},{11,... | collective-permute-start | bytes 3145736 | tf_op jit(solution)/shard_map/ppermute | solution.py:161
  5.4 65.6 %collective-permute-start.3 = (bf16[512,1024]{1,0:T(8,128)(2,1)}, bf16[512,1024]{1,0:T(8,128)(2,1)}, u32[]{:S(2)}, u32[]{:S(2)}) collective-permute-start(bf16[512,1024]{1,0:T(8,128)(2,1)} %bitcast.14), channel_id=1, source_target_pairs={{0,1},{1,0},{2,3},{3,2},{4,5},{5,4},{6,7},{7,6},{9,10},{10,9},{11,... | collective-permute-start | bytes 3145736 | tf_op jit(solution)/shard_map/ppermute | solution.py:162
  7.4 6.6 %collective-permute-start = (bf16[32,512]{1,0:T(8,128)(2,1)}, bf16[32,512]{1,0:T(8,128)(2,1)S(1)}, u32[]{:S(2)}, u32[]{:S(2)}) collective-permute-start(bf16[32,512]{1,0:T(8,128)(2,1)} %own_ref.1), channel_id=1, source_target_pairs={{0,1},{1,0},{2,3},{3,2},{4,5},{5,4},{6,7},{7,6},{8,9},{9,8},{10,11... | collective-permute-start | bytes 98312 | tf_op jit(solution)/shard_map/ppermute | solution.py:164
  9.4 21.1 %collective-permute-start.1 = (bf16[32,512]{1,0:T(8,128)(2,1)}, bf16[32,512]{1,0:T(8,128)(2,1)S(1)}, u32[]{:S(2)}, u32[]{:S(2)}) collective-permute-start(bf16[32,512]{1,0:T(8,128)(2,1)} %own_ref.1), channel_id=1, source_target_pairs={{0,7},{1,2},{2,1},{3,4},{4,3},{5,6},{6,5},{7,0},{8,15},{9,10},{10,... | collective-permute-start | bytes 98312 | tf_op jit(solution)/shard_map/ppermute | solution.py:164
  30.5 0.8 copy-start.2
  89.1 21.3 %copy-start.1 = (bf16[1,1024,512]{2,1,0:T(8,128)(2,1)S(1)}, bf16[1,1024,512]{2,1,0:T(8,128)(2,1)}, u32[]{:S(2)}) copy-start(bf16[1,1024,512]{2,1,0:T(8,128)(2,1)} %param.11) | copy-start | bytes 3145732
